TPU v7x, 128 devices: a whole 4x4x4 slice. The times are simulated.
128 devices in a mesh: req: 16 (over z, x_lo, core), blk: 8 (over y, x_hi).
Axes of the slice: x: 4 (x_hi: 2, x_lo: 2; x = x_hi * 2 + x_lo), y: 4, z: 4, core: 2. Of those that a mesh axis runs over, the one named last changes fastest.
Arguments:
- prefill_rows: bfloat16 [8, 16, 256, 1536], P('blk', 'req'), may hold values from -3 to 3
- decode_rows: bfloat16 [8, 16, 16, 1536], P('blk', 'req'), may hold values from -3 to 3
- cache_pool: bfloat16 [8, 16, 408, 16, 512], P('blk', 'req'), may hold values from -300 to 300
- page_table: int32 [8, 16, 17, 24], P('blk', 'req'), may hold values from 0 to 407, as said below
- lengths: int32 [8, 16, 17], P('blk', 'req'), may hold values from 1 to 383, as said below
- destination: int32 [8, 16, 16], P('blk', 'req'), may hold values from 0 to 15, as said below
- attn_gain: bfloat16 [1536], replicated, may hold values from 0.5 to 1.5
- inproj_weight: bfloat16 [1536, 2048], replicated, may hold values from -0.15625 to 0.15625
- inproj_bias: bfloat16 [2048], replicated, may hold values from -3 to 3
- outproj_weight: bfloat16 [1536, 1536], replicated, may hold values from -0.15625 to 0.15625
- mlp_gain: bfloat16 [1536], replicated, may hold values from 0.5 to 1.5
- gate_up: bfloat16 [1536, 2, 8960], P('req', None, 'blk'), may hold values from -0.15625 to 0.15625
- down_weight: bfloat16 [8960, 1536], P('blk', 'req'), may hold values from -0.0625 to 0.0625
Outputs:
- prefill_out: bfloat16 [8, 16, 256, 1536], P('blk', 'req')
- decode_out: bfloat16 [8, 16, 16, 1536], P('blk', 'req')
- new_cache: bfloat16 [8, 16, 16, 384, 512], P('blk', 'req')
Inputs may be any that keep to these rules, and one draw needn't show every extreme that they name: Each device sends exactly 0 or 2 of its decode requests to each index of req and receives exactly 16; destination minus source index, modulo the size of req, depends only on the blk index and the slot. `lengths`: slot 16 is the prefill request's context. Every device holds a decode request of length 383. `page_table`: on each device a permutation of its 408 pages.
All inputs are finite; a program needn't handle non-finite values.
Results may differ from a plain program's by a relative error of at most 0.024.
Values may be sent and summed in bfloat16 or wider, within the bound.
A program may use at most 192 MiB of HBM per device.

v0:
```python
import math

import jax
import jax.numpy as jnp
from jax import lax
from jax.sharding import PartitionSpec as P

QUERY_HEADS = 12
KEY_VALUE_HEADS = 2
HEAD_SIZE = 128
CAP = 2


rms_eps = 1e-06
rope_base = 1000000.0


def rms_scale(rows, gain_row):
    rows_wide = rows.astype(jnp.float32)
    inverse = lax.rsqrt(jnp.mean(rows_wide * rows_wide, axis=-1, keepdims=True) + rms_eps)
    return (rows_wide * inverse * gain_row.astype(jnp.float32)).astype(jnp.bfloat16)


def apply_rotary(vectors, token_positions):
    head_dim = vectors.shape[-1]
    half_dim = head_dim // 2
    frequency = rope_base ** (-2.0 * jnp.arange(half_dim, dtype=jnp.float32) / head_dim)
    angles = token_positions.astype(jnp.float32)[:, None] * frequency[None, :]
    cosine = jnp.concatenate([jnp.cos(angles), jnp.cos(angles)], axis=-1)[:, None, :]
    sine_table = jnp.concatenate([jnp.sin(angles), jnp.sin(angles)], axis=-1)[:, None, :]
    turned = jnp.concatenate([-vectors[..., half_dim:], vectors[..., :half_dim]], axis=-1)
    return vectors * cosine + turned * sine_table


def project(normed, weight, bias_row, token_positions):
    mixed_batch = jnp.dot(normed, weight, preferred_element_type=jnp.float32) + bias_row.astype(
        jnp.float32
    )
    query_head_width = QUERY_HEADS * HEAD_SIZE
    key_head_width = KEY_VALUE_HEADS * HEAD_SIZE
    query_rows = apply_rotary(
        mixed_batch[:, :query_head_width].reshape(-1, QUERY_HEADS, HEAD_SIZE), token_positions
    )
    key_row_block = apply_rotary(
        mixed_batch[:, query_head_width : query_head_width + key_head_width].reshape(
            -1, KEY_VALUE_HEADS, HEAD_SIZE
        ),
        token_positions,
    )
    value_rows = mixed_batch[:, query_head_width + key_head_width :]
    key_value_pair = jnp.concatenate(
        [key_row_block.reshape(-1, key_head_width), value_rows], axis=-1
    )
    return (
        query_rows.reshape(-1, query_head_width).astype(jnp.bfloat16),
        key_value_pair.astype(jnp.bfloat16),
    )


def attend(query_rows, key_value_pair, allowed):
    batch_count = query_rows.shape[0]
    total_rows = query_rows.shape[1]
    group_width = QUERY_HEADS // KEY_VALUE_HEADS
    key_head_width = KEY_VALUE_HEADS * HEAD_SIZE
    grouped_heads = query_rows.reshape(
        batch_count, total_rows, KEY_VALUE_HEADS, group_width, HEAD_SIZE
    )
    key_row_block = key_value_pair[:, :, :key_head_width].reshape(
        batch_count, -1, KEY_VALUE_HEADS, HEAD_SIZE
    )
    value_rows = key_value_pair[:, :, key_head_width:].reshape(
        batch_count, -1, KEY_VALUE_HEADS, HEAD_SIZE
    )
    scores = jnp.einsum(
        "bqhgd,bkhd->bhgqk", grouped_heads, key_row_block, preferred_element_type=jnp.float32
    ) / math.sqrt(HEAD_SIZE)
    scores = jnp.where(allowed[:, None, None, :, :], scores, -jnp.inf)
    row_max = jnp.max(scores, axis=-1, keepdims=True)
    weights = jnp.exp(scores - row_max)
    weights = (weights / jnp.sum(weights, axis=-1, keepdims=True)).astype(jnp.bfloat16)
    result = jnp.einsum(
        "bhgqk,bkhd->bqhgd", weights, value_rows, preferred_element_type=jnp.float32
    )
    return result.reshape(batch_count, total_rows, QUERY_HEADS * HEAD_SIZE).astype(jnp.bfloat16)


def extend(cache_rows, key_value_pair, lengths_now):
    token_positions = jnp.arange(cache_rows.shape[1], dtype=jnp.int32)[None, :, None]
    limit = lengths_now[:, None, None]
    return jnp.where(
        token_positions < limit,
        cache_rows,
        jnp.where(token_positions == limit, key_value_pair[:, None, :], jnp.zeros_like(cache_rows)),
    )


def shards(
    prefill_rows,
    decode_rows,
    cache_pool,
    page_table,
    lengths,
    destination,
    attn_gain,
    inproj_weight,
    inproj_bias,
    outproj_weight,
    mlp_gain,
    gate_up,
    down_weight,
):
    n_req = lax.axis_size("req")
    own_index = lax.axis_index("req")
    slot_total = destination.shape[2]
    pool_rows = cache_pool[0, 0]
    table_rows = page_table[0, 0]
    width_per_row = pool_rows.shape[-1]
    cache_length = table_rows.shape[1] * pool_rows.shape[1]
    context = pool_rows[table_rows[slot_total]].reshape(cache_length, width_per_row)
    context_length = lengths[0, 0, slot_total]
    slot_ids = jnp.arange(slot_total, dtype=jnp.int32)

    local_down = jnp.transpose(down_weight)[:, None, :]
    all_weights = lax.all_gather(
        jnp.concatenate([gate_up, local_down], axis=1), "req", axis=0, tiled=True
    )

    send_dest = destination[0, 0]
    decode_x = decode_rows[0, 0]
    own_len = lengths[0, 0, :slot_total]
    same_dest = send_dest[None, :] == send_dest[:, None]
    earlier = same_dest & (slot_ids[None, :] < slot_ids[:, None])
    within = jnp.sum(earlier.astype(jnp.int32), axis=1)
    target = send_dest * CAP + within
    flat_slots = jnp.arange(n_req * CAP, dtype=jnp.int32)
    matches = target[None, :] == flat_slots[:, None]
    picked = jnp.sum(jnp.where(matches, slot_ids[None, :], 0), axis=1)
    send_pages = table_rows[picked]
    send_cache = pool_rows[send_pages].reshape(n_req, CAP, cache_length, width_per_row)
    send_x = decode_x[picked].reshape(n_req, CAP, -1)
    send_len = jnp.broadcast_to(own_len[picked].reshape(n_req, CAP, 1), (n_req, CAP, 128))
    recv_x = lax.all_to_all(send_x, "req", split_axis=0, concat_axis=0, tiled=True)
    recv_len = lax.all_to_all(send_len, "req", split_axis=0, concat_axis=0, tiled=True)

    shift = jnp.mod(send_dest - own_index, n_req)
    source = jnp.mod(own_index - shift, n_req)
    order_key = source * slot_total + slot_ids
    rank = jnp.sum((order_key[None, :] < order_key[:, None]).astype(jnp.int32), axis=1)
    chosen = rank[None, :] == slot_ids[:, None]
    arrival_order = jnp.sum(jnp.where(chosen, (source * CAP + within)[None, :], 0), axis=1)

    prefill_x = prefill_rows[0, 0]
    prefill_count = prefill_x.shape[0]
    block_ids = jnp.arange(prefill_count, dtype=jnp.int32)
    cache_ids = jnp.arange(cache_length, dtype=jnp.int32)
    prefill_q, prefill_kv = project(
        rms_scale(prefill_x, attn_gain), inproj_weight, inproj_bias, context_length + block_ids
    )
    key_block = jnp.concatenate([context, prefill_kv], axis=0)
    allowed = jnp.concatenate(
        [
            jnp.broadcast_to(cache_ids[None, :] < context_length, (prefill_count, cache_length)),
            block_ids[None, :] <= block_ids[:, None],
        ],
        axis=1,
    )
    prefill_att = attend(prefill_q[None], key_block[None], allowed[None])[0]
    prefill_res = prefill_x.astype(jnp.float32) + jnp.dot(
        prefill_att, outproj_weight, preferred_element_type=jnp.float32
    )
    all_weights, prefill_res, send_cache = lax.optimization_barrier(
        (all_weights, prefill_res, send_cache)
    )
    recv_cache = lax.all_to_all(send_cache, "req", split_axis=0, concat_axis=0, tiled=True)
    prefill_partial = feed_forward_partial(prefill_res, mlp_gain, all_weights)
    _, recv_cache, recv_x, recv_len = lax.optimization_barrier(
        (prefill_partial, recv_cache, recv_x, recv_len)
    )
    prefill_out = feed_forward_finish(prefill_res, prefill_partial)
    got_cache = recv_cache.reshape(n_req * CAP, cache_length, width_per_row)[arrival_order]
    got_x = recv_x.reshape(n_req * CAP, -1)[arrival_order]
    got_length = recv_len.reshape(n_req * CAP, 128)[arrival_order, 0]

    decode_q, decode_kv = project(
        rms_scale(got_x, attn_gain), inproj_weight, inproj_bias, got_length
    )
    cache_after = extend(got_cache, decode_kv, got_length)
    decode_allowed = (cache_ids[None, :] <= got_length[:, None])[:, None, :]
    decode_att = attend(decode_q[:, None, :], cache_after, decode_allowed)[:, 0]
    decode_res = got_x.astype(jnp.float32) + jnp.dot(
        decode_att, outproj_weight, preferred_element_type=jnp.float32
    )
    decode_out = small_feed_forward(decode_res, mlp_gain, all_weights)
    return (
        prefill_out[None, None],
        decode_out[None, None],
        cache_after[None, None],
    )


def feed_forward_partial(residual, mlp_gain, all_weights):
    mlp_in = rms_scale(residual, mlp_gain)
    gate_and_up = jnp.einsum(
        "nd,dkf->nkf",
        lax.all_gather(mlp_in, "blk", axis=0, tiled=True),
        all_weights[:, :2, :],
        preferred_element_type=jnp.float32,
    )
    hidden = (jax.nn.silu(gate_and_up[:, 0, :]) * gate_and_up[:, 1, :]).astype(jnp.bfloat16)
    return jnp.einsum(
        "nf,df->nd", hidden, all_weights[:, 2, :], preferred_element_type=jnp.float32
    ).astype(jnp.bfloat16)


def small_feed_forward(residual, mlp_gain, all_weights):
    n_blk = lax.axis_size("blk")
    rows = residual.shape[0]
    mlp_in = rms_scale(residual, mlp_gain)
    spread = jnp.broadcast_to(mlp_in[None], (n_blk,) + mlp_in.shape)
    gathered = lax.all_to_all(spread, "blk", split_axis=0, concat_axis=0, tiled=True)
    gate_and_up = jnp.einsum(
        "nd,dkf->nkf",
        gathered.reshape(n_blk * rows, -1),
        all_weights[:, :2, :],
        preferred_element_type=jnp.float32,
    )
    hidden = (jax.nn.silu(gate_and_up[:, 0, :]) * gate_and_up[:, 1, :]).astype(jnp.bfloat16)
    partial = jnp.einsum(
        "nf,df->nd", hidden, all_weights[:, 2, :], preferred_element_type=jnp.float32
    ).astype(jnp.bfloat16)
    returned = lax.all_to_all(
        partial.reshape(n_blk, rows, -1), "blk", split_axis=0, concat_axis=0, tiled=True
    )
    mlp_rows = jnp.sum(returned.astype(jnp.float32), axis=0)
    return (residual + mlp_rows).astype(jnp.bfloat16)


def feed_forward_finish(residual, partial):
    mlp_rows = lax.psum_scatter(partial, "blk", scatter_dimension=0, tiled=True)
    return (residual + mlp_rows.astype(jnp.float32)).astype(jnp.bfloat16)


def solution(mesh):
    return jax.shard_map(
        shards,
        mesh=mesh,
        in_specs=(
            P("blk", "req", None, None),
            P("blk", "req", None, None),
            P("blk", "req", None, None, None),
            P("blk", "req", None, None),
            P("blk", "req", None),
            P("blk", "req", None),
            P(),
            P(),
            P(),
            P(),
            P(),
            P("req", None, "blk"),
            P("blk", "req"),
        ),
        out_specs=(
            P("blk", "req", None, None),
            P("blk", "req", None, None),
            P("blk", "req", None, None, None),
        ),
        check_vma=False,
    )
```

profile of v0, /device:TPU:0, one launch (start us, length us, event | category | flops | bytes accessed | tf_op | source)
XLA Modules:
  0.0 391.3 jit_solution(3170162230535409527)
XLA Ops:
  7.2 1.1 copy.72
  8.3 1.9 pad_maximum_fusion
  10.2 0.7 convert_element_type.137
  10.9 0.7 convert_element_type.139
  11.6 1.4 fusion.20
  13.0 4.9 %convolution_add_fusion.1 = f32[256,2048]{1,0:T(8,128)S(1)} fusion(bf16[1536,2048]{1,0:T(8,128)(2,1)} %param.20, f32[2048]{0:T(1024)S(1)} %convert_element_type.139, bf16[1,1,256,1536]{3,2,1,0:T(8,128)(2,1)} %param.13, f32[1536]{0:T(1024)S(1)} %convert_element_type.137, f32[256]{0:T(256)S(1)} %add_rsqrt_fusion.1), kind=kOutput, calls=%fused_computation.32 | convolution fusion | flops 1612709888 | bytes 9190400 | tf_op jit(solution)/shard_map/dot_general | solution.py:36
  18.0 1.3 slice.135
  19.3 0.6 slice.88
  19.9 0.7 add_convert_fusion.3
  20.5 0.3 multiply_cosine_fusion
  20.9 0.7 copy.74
  21.7 0.7 copy.73
  22.5 3.5 gather_fusion
  26.0 0.3 slice_negate_fusion.1
  26.3 1.3 maximum_multiply_fusion.1
  27.6 1.0 mul.264
  28.7 0.8 fusion.64
  29.7 3.1 copy.78
  32.8 1.5 slice_negate_fusion
  34.3 1.3 maximum_multiply_fusion
  35.6 3.1 copy.79
  38.6 1.3 mul.270
  39.9 3.0 copy.77
  42.9 2.2 add_convert_fusion.1
  45.4 1.2 copy.75
  47.0 0.6 gather_fusion.1
  47.7 22.8 %gather_fusion.2 = bf16[768,16,512]{2,1,0:T(8,128)(2,1)} fusion(bf16[408,16,512]{2,1,0:T(8,128)(2,1)} %bitcast.186, s32[1024]{0:T(1024)S(1)} %pad_clamp_fusion.2), kind=kCustom, calls=%fused_computation.2 | custom fusion | bytes 25168896 | tf_op jit(solution)/shard_map/gather | solution.py:139
  70.5 0.7 iota_compare_fusion.7
  71.4 1.3 fusion.7
  72.7 1.6 fusion.1
  74.4 2.5 fusion.23
  76.9 1.4 convolution_add_fusion
  78.6 1.1 multiply_convert_fusion
  79.7 0.7 gather_fusion.4
  80.5 0.7 broadcast_in_dim.103
  81.2 6.4 %all-to-all-start.2 = ((s32[16,2,128]{2,1,0:T(2,128)}), s32[16,2,128]{2,1,0:T(2,128)S(1)}, u32[]{:S(2)}, u32[]{:S(2)}) async-start(s32[16,2,128]{2,1,0:T(2,128)} %broadcast_in_dim.103), calls=%async_computation.3 | async-start | bytes 32768 | tf_op jit(solution)/shard_map/all_to_all | solution.py:143
  87.6 0.6 gather_fusion.3
  88.3 5.4 %all-to-all-done.2 = s32[16,2,128]{2,1,0:T(2,128)S(1)} async-done(((s32[16,2,128]{2,1,0:T(2,128)}), s32[16,2,128]{2,1,0:T(2,128)S(1)}, u32[]{:S(2)}, u32[]{:S(2)}) %all-to-all-start.2) | async-done | bytes 16416 | tf_op jit(solution)/shard_map/all_to_all | solution.py:143
  93.7 10.2 %all_to_all.25 = bf16[16,2,1536]{2,1,0:T(2,128)(2,1)S(1)} all-to-all(bf16[16,2,1536]{2,1,0:T(2,128)(2,1)S(1)} %reshape.462), channel_id=1, replica_groups=mesh['req'=16,'blk'=8] {'req'}, dimensions={0} | all-to-all | bytes 196608 | tf_op jit(solution)/shard_map/all_to_all | solution.py:142
  103.9 4.9 %all-to-all-start = ((bf16[16,2,384,512]{3,2,1,0:T(8,128)(2,1)}), bf16[16,2,384,512]{3,2,1,0:T(8,128)(2,1)}, u32[]{:S(2)}, u32[]{:S(2)}) async-start(bf16[16,2,384,512]{3,2,1,0:T(8,128)(2,1)} %bitcast.182), calls=%async_computation.1 | async-start | bytes 25165824 | tf_op jit(solution)/shard_map/all_to_all | solution.py:174
  108.9 14.2 %copy.84 = bf16[1536,3,1120]{0,2,1:T(8,128)(2,1)} copy(bf16[1536,3,1120]{2,0,1:T(8,128)(2,1)} %all-gather.3.cloned.1.call-done) | data formatting | bytes 20643840 | tf_op jit(solution)/shard_map/optimization_barrier | solution.py:171
  123.2 82.9 %all-gather.5.cloned.1.call-done = bf16[2048,1536]{1,0:T(8,128)(2,1)} async-done(((bf16[256,1536]{1,0:T(8,128)(2,1)}), bf16[2048,1536]{1,0:T(8,128)(2,1)}) %all-gather.5.cloned.1.call-update) | async-done | bytes 6291472 | tf_op jit(solution)/shard_map/all_gather | solution.py:205
  206.0 20.5 %fusion.2 = f32[2048,2,1120]{0,2,1:T(8,128)} fusion(bf16[2048,1536]{1,0:T(8,128)(2,1)} %all-gather.5.cloned.1.call-done, bf16[1536,3,1120]{0,2,1:T(8,128)(2,1)} %copy.84), kind=kOutput, calls=%fused_computation.16 | convolution fusion | flops 14092861440 | bytes 31522816 | tf_op jit(solution)/shard_map/nd,dkf->nkf/dot_general | solution.py:203
  226.5 15.0 %convolution_convert_fusion = bf16[2048,1536]{1,0:T(8,128)(2,1)} fusion(f32[2048,2,1120]{0,2,1:T(8,128)} %fusion.2, bf16[1536,3,1120]{2,0,1:T(8,128)(2,1)} %all-gather.3.cloned.1.call-done), kind=kOutput, calls=%fused_computation.13 | convolution fusion | flops 7063339008 | bytes 28180480 | tf_op jit(solution)/shard_map/nf,df->nd/dot_general | solution.py:210
  241.9 57.7 %all-to-all-done = bf16[16,2,384,512]{3,2,1,0:T(8,128)(2,1)} async-done(((bf16[16,2,384,512]{3,2,1,0:T(8,128)(2,1)}), bf16[16,2,384,512]{3,2,1,0:T(8,128)(2,1)}, u32[]{:S(2)}, u32[]{:S(2)}) %all-to-all-start) | async-done | bytes 12582944 | tf_op jit(solution)/shard_map/all_to_all | solution.py:174
  299.6 0.6 gather_fusion.5
  300.4 4.0 %convolution_add_fusion.3 = f32[16,2048]{1,0:T(8,128)S(1)} fusion(bf16[1536,2048]{1,0:T(8,128)(2,1)} %param.20, f32[2048]{0:T(1024)S(1)} %convert_element_type.139, bf16[16,1536]{1,0:T(8,128)(2,1)S(1)} %gather_fusion.5, f32[1536]{0:T(1024)S(1)} %convert_element_type.137, f32[16]{0:T(128)S(1)} %add_rsqrt_fusion.3), kind=kOutput, calls=%fused_computation.37 | convolution fusion | flops 100794368 | bytes 6486080 | tf_op jit(solution)/shard_map/dot_general | solution.py:36
  304.5 0.7 gather_fusion.6
  305.1 8.3 %gather_fusion.7 = bf16[16,384,512]{2,1,0:T(8,128)(2,1)} fusion(bf16[32,384,512]{2,1,0:T(8,128)(2,1)} %bitcast.41, s32[1024]{0:T(1024)S(1)} %pad_clamp_fusion), kind=kCustom, calls=%fused_computation.7 | custom fusion | bytes 12582976 | tf_op jit(solution)/shard_map/gather | solution.py:180
  314.4 6.2 %select_select_fusion = bf16[16,384,512]{2,1,0:T(8,128)(2,1)S(1)} fusion(bf16[16,384,512]{2,1,0:T(8,128)(2,1)} %gather_fusion.7, pred[16,384]{1,0:T(8,128)(4,1)S(1)} %get-tuple-element.37, pred[16,384]{1,0:T(8,128)(4,1)S(1)} %get-tuple-element.38, bf16[16,512]{1,0:T(8,128)(2,1)S(1)} %pad_maximum_fusion.3), kind=kLoop, calls=%fused_computation.18 | loop fusion | flops 6291456 | bytes 12611584 | tf_op jit(solution)/shard_map/jit(_where)/select_n | solution.py:90
  320.6 3.5 fusion.63
  324.0 4.6 %copy.86 = bf16[16,384,256]{1,2,0:T(8,128)(2,1)} copy(bf16[16,384,256]{2,1,0:T(8,128)(2,1)} %get-tuple-element.20) | data formatting | bytes 6291456 | tf_op jit(solution)/shard_map/slice | solution.py:68
  328.7 4.7 %copy.85 = bf16[16,384,256]{1,2,0:T(8,128)(2,1)} copy(bf16[16,384,256]{2,1,0:T(8,128)(2,1)} %get-tuple-element.21) | data formatting | bytes 6291456 | tf_op jit(solution)/shard_map/slice | solution.py:71
  333.4 3.1 fusion.65
  336.7 3.1 fusion.29
  339.9 3.2 multiply_reduce_fusion.1
  343.3 16.7 %all_to_all.26 = bf16[8,16,1536]{2,1,0:T(8,128)(2,1)S(1)} all-to-all(bf16[8,16,1536]{2,1,0:T(8,128)(2,1)S(1)} %broadcast_in_dim.116), channel_id=1, replica_groups=mesh['req'=16,'blk'=8] {'blk'}, dimensions={0} | all-to-all | bytes 786432 | tf_op jit(solution)/shard_map/all_to_all | solution.py:220
  359.9 4.9 %fusion.4 = f32[128,2,1120]{0,2,1:T(8,128)S(1)} fusion(bf16[128,1536,1]{1,0,2:T(8,128)(2,1)S(1)} %bitcast.202, bf16[1536,3,1120]{0,2,1:T(8,128)(2,1)} %copy.84), kind=kOutput, calls=%fused_computation.19 | convolution fusion | flops 880803840 | bytes 8421376 | tf_op jit(solution)/shard_map/nd,dkf->nkf/dot_general | solution.py:221
  364.9 4.1 %fusion.17 = bf16[128,1536]{1,0:T(8,128)(2,1)} fusion(bf16[1536,3,1120]{2,0,1:T(8,128)(2,1)} %all-gather.3.cloned.1.call-done, f32[128,2,1120]{0,2,1:T(8,128)S(1)} %fusion.4), kind=kOutput, calls=%fused_computation.33 | convolution fusion | flops 441458688 | bytes 5079040 | tf_op jit(solution)/shard_map/nf,df->nd/dot_general | solution.py:228
  368.9 3.5 all-to-all-start.4
  372.4 7.6 %bitcast_select_fusion.1 = bf16[1,1,16,384,512]{4,3,2,1,0:T(8,128)(2,1)} fusion(bf16[16,384,512]{2,1,0:T(8,128)(2,1)} %gather_fusion.7, pred[16,384]{1,0:T(8,128)(4,1)S(1)} %get-tuple-element.37, pred[16,384]{1,0:T(8,128)(4,1)S(1)} %get-tuple-element.38, bf16[16,512]{1,0:T(8,128)(2,1)S(1)} %pad_maximum_fusion.3), kind=kLoop, calls=%fused_computation.15 | loop fusion | flops 6291456 | bytes 12611584 | tf_op jit(solution)/shard_map/jit(_where)/select_n | solution.py:90
  380.0 1.8 all-to-all-done.4
  381.9 0.6 fusion.46
  382.5 2.2 fusion.30
  (93 shorter events, 3.9 us)
Async XLA Ops:
  7.2 80.5 %copy-start = (bf16[1,1,16,1536]{3,2,1,0:T(8,128)(2,1)S(1)}, bf16[1,1,16,1536]{3,2,1,0:T(8,128)(2,1)}, u32[]{:S(2)}) copy-start(bf16[1,1,16,1536]{3,2,1,0:T(8,128)(2,1)} %param.14) | copy-start | bytes 147460
  7.2 71.2 %all-gather.3.cloned.1.call-start = ((), (), s32[]{:S(2)}) async-start(), calls=%async_computation.6 | async-start | bytes 11280384 | tf_op jit(solution)/shard_map/all_gather | solution.py:124
  10.2 195.9 %all-gather.5.cloned.1.call-start = ((), (), s32[]{:S(2)}) async-start(), calls=%async_computation.7 | async-start | bytes 7077888 | tf_op jit(solution)/shard_map/all_gather | solution.py:205
  13.0 6.3 %copy-start.6 = (s32[1,1,17]{2,1,0:T(1,128)S(1)}, s32[1,1,17]{2,1,0:T(1,128)}, u32[]{:S(2)}) copy-start(s32[1,1,17]{2,1,0:T(1,128)} %param.17) | copy-start | bytes 208
  13.0 9.5 %copy-start.3 = (s32[1,1,17,24]{3,1,2,0:T(1,128)S(1)}, s32[1,1,17,24]{3,1,2,0:T(1,128)}, u32[]{:S(2)}) copy-start(s32[1,1,17,24]{3,1,2,0:T(1,128)} %param.16) | copy-start | bytes 4900
  38.6 8.0 %copy-start.5 = (s32[1,1,16]{2,1,0:T(1,128)S(1)}, s32[1,1,16]{2,1,0:T(1,128)}, u32[]{:S(2)}) copy-start(s32[1,1,16]{2,1,0:T(1,128)} %param.18) | copy-start | bytes 196
  47.6 22.8 %copy-start.4 = (bf16[1536]{0:T(1024)(128)(2,1)S(1)}, bf16[1536]{0:T(1024)(128)(2,1)}, u32[]{:S(2)}) copy-start(bf16[1536]{0:T(1024)(128)(2,1)} %param.23) | copy-start | bytes 9220
  72.7 4.2 %slice-start = ((s8[4718592]{0:T(1024)(128)(4,1)}), s8[524288]{0:T(1024)(128)(4,1)S(1)}, s32[]{:S(2)}) async-start(s8[4718592]{0:T(1024)(128)(4,1)} %bitcast.183), calls=%async_computation.9 | async-start | bytes 1048576
  74.3 2.6 slice-start.1
  74.3 2.5 copy-start.2
  76.9 2.8 copy-start.7
  81.2 12.5 %all-to-all-start.2 = ((s32[16,2,128]{2,1,0:T(2,128)}), s32[16,2,128]{2,1,0:T(2,128)S(1)}, u32[]{:S(2)}, u32[]{:S(2)}) async-start(s32[16,2,128]{2,1,0:T(2,128)} %broadcast_in_dim.103), calls=%async_computation.3 | async-start | bytes 32768 | tf_op jit(solution)/shard_map/all_to_all | solution.py:143
  103.9 195.7 %all-to-all-start = ((bf16[16,2,384,512]{3,2,1,0:T(8,128)(2,1)}), bf16[16,2,384,512]{3,2,1,0:T(8,128)(2,1)}, u32[]{:S(2)}, u32[]{:S(2)}) async-start(bf16[16,2,384,512]{3,2,1,0:T(8,128)(2,1)} %bitcast.182), calls=%async_computation.1 | async-start | bytes 25165824 | tf_op jit(solution)/shard_map/all_to_all | solution.py:174
  108.9 273.6 %reduce-scatter.2.cloned.1.call-start = ((), (), s32[]{:S(2)}) async-start(), calls=%async_computation.8 | async-start | bytes 7077888 | tf_op jit(solution)/shard_map/reduce_scatter | solution.py:239
  368.9 12.9 %all-to-all-start.4 = ((bf16[8,16,1536]{2,1,0:T(8,128)(2,1)}), bf16[8,16,1536]{2,1,0:T(8,128)(2,1)S(1)}, u32[]{:S(2)}, u32[]{:S(2)}) async-start(bf16[8,16,1536]{2,1,0:T(8,128)(2,1)} %bitcast.52), calls=%async_computation.5 | async-start | bytes 786432 | tf_op jit(solution)/shard_map/all_to_all | solution.py:231
  372.4 12.3 %copy-start.1 = (bf16[1,1,16,1536]{3,2,1,0:T(8,128)(2,1)S(1)}, bf16[1,1,16,1536]{3,2,1,0:T(8,128)(2,1)}, u32[]{:S(2)}) copy-start(bf16[1,1,16,1536]{3,2,1,0:T(8,128)(2,1)} %param.14) | copy-start | bytes 147460
Sparse Core Ops, SparseCore 0:
  10.3 65.1 all-gather.2
  79.8 126.2 all-gather.4
  241.7 116.9 reduce-scatter.1
where the time goes:
time: 393 us; the launch traced here: 391 us
  waiting for transfers between devices  148 us (38%)
  local copies, waits for them, and re-layouts  84.6 us (22%)
  matrix products  68 us (17%)
  other arithmetic  34.7 us (9%)
  blocking collectives  26.9 us (7%)
  starting transfers between devices  14.9 us (4%)
  between operations  14.3 us (4%)
    all_gather x1, waiting for transfers between devices, feed_forward_partial(): lax.all_gather(mlp_in, 'blk', axis=0, tiled=True)  82.9 us
    all_to_all x1, waiting for transfers between devices, shards(): lax.all_to_all(send_cache, 'req', split_axis=0, concat_axis=0, tiled=True)  57.7 us
    gather x1, local copies, waits for them, and re-layouts, shards(): pool_rows[send_pages].reshape(n_req, CAP, cache_length, width_per_row)  22.8 us
    dot_general x1, matrix products, feed_forward_partial(): jnp.einsum('nd,dkf->nkf', lax.all_gather(mlp_in, 'blk', axis=0, tiled=Tru...  20.5 us
    all_to_all x1, blocking collectives, small_feed_forward(): lax.all_to_all(spread, 'blk', split_axis=0, concat_axis=0, tiled=True)  16.7 us
    dot_general x1, matrix products, feed_forward_partial(): jnp.einsum('nf,df->nd', hidden, all_weights[:, 2, :], preferred_element_t...  15 us
    optimization_barrier x1, local copies, waits for them, and re-layouts, shards(): lax.optimization_barrier((all_weights, prefill_res, send_cache))  14.2 us
    select_n x2, other arithmetic, extend(): jnp.where(token_positions < limit, cache_rows, jnp.where(token_positions...  13.8 us
  transfers between devices with their start and end apart: 6, of which 4 were waited for; matrix products, arithmetic and copies ran while one was open for 46% of the time, Pallas kernels for 0%

commit v1 on v0

--- a/solution.py
+++ b/solution.py
@@ -3,6 +3,8 @@
 import jax
 import jax.numpy as jnp
 from jax import lax
+from jax.experimental import pallas as pl
+from jax.experimental.pallas import tpu as pltpu
 from jax.sharding import PartitionSpec as P
 
 QUERY_HEADS = 12
@@ -82,6 +84,71 @@
         "bhgqk,bkhd->bqhgd", weights, value_rows, preferred_element_type=jnp.float32
     )
     return result.reshape(batch_count, total_rows, QUERY_HEADS * HEAD_SIZE).astype(jnp.bfloat16)
+
+
+def decode_kernel(order_ref, length_ref, cache_ref, kv_ref, q_ref, new_ref, att_ref):
+    limit = length_ref[pl.program_id(0)]
+    rows = cache_ref[...]
+    positions = lax.broadcasted_iota(jnp.int32, rows.shape, 0)
+    extended = jnp.where(
+        positions < limit,
+        rows,
+        jnp.where(positions == limit, kv_ref[...], jnp.zeros_like(rows)),
+    )
+    new_ref[...] = extended
+    group_width = QUERY_HEADS // KEY_VALUE_HEADS
+    key_head_width = KEY_VALUE_HEADS * HEAD_SIZE
+    key_ids = lax.broadcasted_iota(jnp.int32, (group_width, rows.shape[0]), 1)
+    for head in range(KEY_VALUE_HEADS):
+        keys = extended[:, head * HEAD_SIZE : (head + 1) * HEAD_SIZE]
+        values = extended[:, key_head_width + head * HEAD_SIZE : key_head_width + (head + 1) * HEAD_SIZE]
+        scores = lax.dot_general(
+            q_ref[head], keys, (((1,), (1,)), ((), ())), preferred_element_type=jnp.float32
+        ) / math.sqrt(HEAD_SIZE)
+        scores = jnp.where(key_ids <= limit, scores, -jnp.inf)
+        weights = jnp.exp(scores - jnp.max(scores, axis=1, keepdims=True))
+        weights = (weights / jnp.sum(weights, axis=1, keepdims=True)).astype(jnp.bfloat16)
+        att_ref[head] = jnp.dot(weights, values, preferred_element_type=jnp.float32).astype(
+            jnp.bfloat16
+        )
+
+
+def decode_attend(arrival_order, got_length, recv_cache, decode_kv, decode_q):
+    count = arrival_order.shape[0]
+    cache_length, width_per_row = recv_cache.shape[1:]
+    group_width = QUERY_HEADS // KEY_VALUE_HEADS
+    order = jnp.clip(arrival_order, 0, recv_cache.shape[0] - 1)
+    new_cache, attended = pl.pallas_call(
+        decode_kernel,
+        grid_spec=pltpu.PrefetchScalarGridSpec(
+            num_scalar_prefetch=2,
+            grid=(count,),
+            in_specs=[
+                pl.BlockSpec((None, cache_length, width_per_row), lambda p, o, n: (o[p], 0, 0)),
+                pl.BlockSpec((None, 1, width_per_row), lambda p, o, n: (p, 0, 0)),
+                pl.BlockSpec(
+                    (None, KEY_VALUE_HEADS, group_width, HEAD_SIZE), lambda p, o, n: (p, 0, 0, 0)
+                ),
+            ],
+            out_specs=[
+                pl.BlockSpec((None, cache_length, width_per_row), lambda p, o, n: (p, 0, 0)),
+                pl.BlockSpec(
+                    (None, KEY_VALUE_HEADS, group_width, HEAD_SIZE), lambda p, o, n: (p, 0, 0, 0)
+                ),
+            ],
+        ),
+        out_shape=[
+            jax.ShapeDtypeStruct((count, cache_length, width_per_row), jnp.bfloat16),
+            jax.ShapeDtypeStruct((count, KEY_VALUE_HEADS, group_width, HEAD_SIZE), jnp.bfloat16),
+        ],
+    )(
+        order,
+        got_length,
+        recv_cache,
+        decode_kv.reshape(count, 1, width_per_row),
+        decode_q.reshape(count, KEY_VALUE_HEADS, group_width, HEAD_SIZE),
+    )
+    return new_cache, attended.reshape(count, QUERY_HEADS * HEAD_SIZE)
 
 
 def extend(cache_rows, key_value_pair, lengths_now):
@@ -177,16 +244,19 @@
         (prefill_partial, recv_cache, recv_x, recv_len)
     )
     prefill_out = feed_forward_finish(prefill_res, prefill_partial)
-    got_cache = recv_cache.reshape(n_req * CAP, cache_length, width_per_row)[arrival_order]
     got_x = recv_x.reshape(n_req * CAP, -1)[arrival_order]
     got_length = recv_len.reshape(n_req * CAP, 128)[arrival_order, 0]
 
     decode_q, decode_kv = project(
         rms_scale(got_x, attn_gain), inproj_weight, inproj_bias, got_length
     )
-    cache_after = extend(got_cache, decode_kv, got_length)
-    decode_allowed = (cache_ids[None, :] <= got_length[:, None])[:, None, :]
-    decode_att = attend(decode_q[:, None, :], cache_after, decode_allowed)[:, 0]
+    cache_after, decode_att = decode_attend(
+        arrival_order,
+        got_length,
+        recv_cache.reshape(n_req * CAP, cache_length, width_per_row),
+        decode_kv,
+        decode_q,
+    )
     decode_res = got_x.astype(jnp.float32) + jnp.dot(
         decode_att, outproj_weight, preferred_element_type=jnp.float32
     )

time: 393 us -> 388 us (0.987)
  local copies, waits for them, and re-layouts: 84.6 us -> 57.1 us
  waiting for transfers between devices: 148 us -> 167 us
  Pallas kernels: 0 us -> 17 us
  other arithmetic: 34.7 us -> 22.2 us
  matrix products: 68 us -> 60.8 us
  blocking collectives: 26.9 us -> 33.2 us
    pallas_call x0 -> x1, Pallas kernels: none -> 17 us  [decode_attend(): pl.pallas_call(decode_kernel, grid_spec=pltpu.PrefetchScalarGridSpec(num_...]
    select_n x2 -> x1, other arithmetic: 13.8 us -> 0.01 us  [shards(): got_x = recv_x.reshape(n_req * CAP, -1)[arrival_order]]
    all_to_all x1, waiting for transfers between devices: 57.7 us -> 67.2 us  [shards(): lax.all_to_all(send_cache, 'req', split_axis=0, concat_axis=0, tiled=True)]
    gather x1 -> x0, local copies, waits for them, and re-layouts: 8.25 us -> none  [shards(): recv_cache.reshape(n_req * CAP, cache_length, width_per_row)[arrival_order]]
    slice x4 -> x2, local copies, waits for them, and re-layouts: 9.08 us -> 0.98 us  [attend(): key_value_pair[:, :, :key_head_width]]
    all_gather x1, waiting for transfers between devices: 82.9 us -> 90.2 us  [feed_forward_partial(): lax.all_gather(mlp_in, 'blk', axis=0, tiled=True)]
    mul x6, local copies, waits for them, and re-layouts: 8.4 us -> 3.25 us  [apply_rotary(): return vectors * cosine + turned * sine_table]
    all_gather x1, waiting for transfers between devices: 0.02 us -> 5.06 us  [shards(): lax.all_gather(jnp.concatenate([gate_up, local_down], axis=1), 'req', axi...]
  transfers between devices with their start and end apart: 6 -> 6, of which waited for: 4 -> 4; matrix products, arithmetic and copies ran while one was open for 46% -> 34% of each run, Pallas kernels for 0% -> 4%
where the time goes in v1:
time: 388 us; the launch traced here: 386 us
  waiting for transfers between devices  167 us (43%)
  matrix products  60.8 us (16%)
  local copies, waits for them, and re-layouts  57.1 us (15%)
  blocking collectives  33.2 us (9%)
  other arithmetic  22.2 us (6%)
  Pallas kernels  17 us (4%)
  starting transfers between devices  14.4 us (4%)
  between operations  14.4 us (4%)
    all_gather x1, waiting for transfers between devices, feed_forward_partial(): lax.all_gather(mlp_in, 'blk', axis=0, tiled=True)  90.2 us
    all_to_all x1, waiting for transfers between devices, shards(): lax.all_to_all(send_cache, 'req', split_axis=0, concat_axis=0, tiled=True)  67.2 us
    gather x1, local copies, waits for them, and re-layouts, shards(): pool_rows[send_pages].reshape(n_req, CAP, cache_length, width_per_row)  22.7 us
    all_to_all x1, blocking collectives, small_feed_forward(): lax.all_to_all(spread, 'blk', split_axis=0, concat_axis=0, tiled=True)  21 us
    dot_general x1, matrix products, feed_forward_partial(): jnp.einsum('nd,dkf->nkf', lax.all_gather(mlp_in, 'blk', axis=0, tiled=Tru...  20.5 us
    pallas_call x1, Pallas kernels, decode_attend(): pl.pallas_call(decode_kernel, grid_spec=pltpu.PrefetchScalarGridSpec(num_...  17 us
    dot_general x1, matrix products, feed_forward_partial(): jnp.einsum('nf,df->nd', hidden, all_weights[:, 2, :], preferred_element_t...  15 us
    optimization_barrier x1, local copies, waits for them, and re-layouts, shards(): lax.optimization_barrier((all_weights, prefill_res, send_cache))  14.3 us
  transfers between devices with their start and end apart: 6, of which 4 were waited for; matrix products, arithmetic and copies ran while one was open for 34% of the time, Pallas kernels for 4%

profile of v1, /device:TPU:0, one launch (start us, length us, event | category | flops | bytes accessed | tf_op | source)
XLA Modules:
  0.0 386.4 jit_solution(14645063567159313178)
XLA Ops:
  7.2 1.1 copy.67
  8.3 1.9 pad_maximum_fusion
  10.2 0.7 convert_element_type.122
  10.9 0.7 convert_element_type.124
  11.6 1.4 fusion.20
  13.0 4.9 %convolution_add_fusion.1 = f32[256,2048]{1,0:T(8,128)S(1)} fusion(bf16[1536,2048]{1,0:T(8,128)(2,1)} %param.20, f32[2048]{0:T(1024)S(1)} %convert_element_type.124, bf16[1,1,256,1536]{3,2,1,0:T(8,128)(2,1)} %param.13, f32[1536]{0:T(1024)S(1)} %convert_element_type.122, f32[256]{0:T(256)S(1)} %add_rsqrt_fusion.1), kind=kOutput, calls=%fused_computation.29 | convolution fusion | flops 1612709888 | bytes 9190400 | tf_op jit(solution)/shard_map/dot_general | solution.py:38
  18.0 1.3 copy-done.2
  19.2 0.6 slice.82
  19.8 0.7 add_convert_fusion.3
  20.5 0.3 multiply_cosine_fusion
  20.9 0.6 copy-done.4
  21.9 3.6 gather_fusion
  25.4 0.3 slice_negate_fusion.1
  25.8 0.4 maximum_multiply_fusion.1
  26.2 1.0 fusion.34
  27.3 0.8 fusion.58
  28.3 0.5 copy.73
  28.9 1.0 maximum_multiply_fusion
  29.9 0.5 copy.74
  30.4 1.0 mul.270
  31.4 1.6 copy.72
  33.1 2.3 add_convert_fusion.1
  35.3 0.3 copy.75
  35.6 1.2 copy.70
  36.8 0.9 convert_reduce_fusion.2
  37.7 0.7 iota_add_fusion
  38.4 0.7 multiply_add_fusion
  39.2 0.6 gather_fusion.1
  39.9 22.7 %gather_fusion.2 = bf16[768,16,512]{2,1,0:T(8,128)(2,1)} fusion(bf16[408,16,512]{2,1,0:T(8,128)(2,1)} %bitcast.171, s32[1024]{0:T(1024)S(1)} %pad_clamp_fusion.2), kind=kCustom, calls=%fused_computation.2 | custom fusion | bytes 25168896 | tf_op jit(solution)/shard_map/gather | solution.py:206
  62.6 0.7 iota_compare_fusion.4
  63.5 1.3 fusion.7
  64.8 1.6 fusion.1
  66.5 2.5 fusion.23
  69.0 1.4 convolution_add_fusion
  70.4 5.1 %all-gather.3.cloned.1.call-done = bf16[1536,3,1120]{2,0,1:T(8,128)(2,1)} async-done(((bf16[96,3,1120]{2,0,1:T(8,128)(2,1)}), bf16[1536,3,1120]{2,0,1:T(8,128)(2,1)}) %all-gather.3.cloned.1.call-update) | async-done | bytes 10321936 | tf_op jit(solution)/shard_map/all_gather | solution.py:191
  75.7 1.1 multiply_convert_fusion
  76.8 0.7 gather_fusion.4
  77.6 0.7 broadcast_in_dim.63
  78.3 5.1 %all-to-all-start.2 = ((s32[16,2,128]{2,1,0:T(2,128)}), s32[16,2,128]{2,1,0:T(2,128)S(1)}, u32[]{:S(2)}, u32[]{:S(2)}) async-start(s32[16,2,128]{2,1,0:T(2,128)} %broadcast_in_dim.63), calls=%async_computation.3 | async-start | bytes 32768 | tf_op jit(solution)/shard_map/all_to_all | solution.py:210
  83.4 0.6 gather_fusion.3
  84.0 0.7 reshape.376
  84.7 4.7 %all-to-all-done.2 = s32[16,2,128]{2,1,0:T(2,128)S(1)} async-done(((s32[16,2,128]{2,1,0:T(2,128)}), s32[16,2,128]{2,1,0:T(2,128)S(1)}, u32[]{:S(2)}, u32[]{:S(2)}) %all-to-all-start.2) | async-done | bytes 16416 | tf_op jit(solution)/shard_map/all_to_all | solution.py:210
  89.5 3.5 all-to-all-start.1
  93.0 14.3 %copy.79 = bf16[1536,3,1120]{0,2,1:T(8,128)(2,1)} copy(bf16[1536,3,1120]{2,0,1:T(8,128)(2,1)} %all-gather.3.cloned.1.call-done) | data formatting | bytes 20643840 | tf_op jit(solution)/shard_map/optimization_barrier | solution.py:238
  107.3 5.7 %all-to-all-start = ((bf16[16,2,384,512]{3,2,1,0:T(8,128)(2,1)}), bf16[16,2,384,512]{3,2,1,0:T(8,128)(2,1)}, u32[]{:S(2)}, u32[]{:S(2)}) async-start(bf16[16,2,384,512]{3,2,1,0:T(8,128)(2,1)} %bitcast.167), calls=%async_computation.1 | async-start | bytes 25165824 | tf_op jit(solution)/shard_map/all_to_all | solution.py:241
  113.0 90.2 %all-gather.5.cloned.1.call-done = bf16[2048,1536]{1,0:T(8,128)(2,1)} async-done(((bf16[256,1536]{1,0:T(8,128)(2,1)}), bf16[2048,1536]{1,0:T(8,128)(2,1)}) %all-gather.5.cloned.1.call-update) | async-done | bytes 6291472 | tf_op jit(solution)/shard_map/all_gather | solution.py:275
  203.3 20.5 %fusion.2 = f32[2048,2,1120]{0,2,1:T(8,128)} fusion(bf16[2048,1536]{1,0:T(8,128)(2,1)} %all-gather.5.cloned.1.call-done, bf16[1536,3,1120]{0,2,1:T(8,128)(2,1)} %copy.79), kind=kOutput, calls=%fused_computation.14 | convolution fusion | flops 14092861440 | bytes 31522816 | tf_op jit(solution)/shard_map/nd,dkf->nkf/dot_general | solution.py:273
  223.7 15.0 %convolution_convert_fusion = bf16[2048,1536]{1,0:T(8,128)(2,1)} fusion(f32[2048,2,1120]{0,2,1:T(8,128)} %fusion.2, bf16[1536,3,1120]{2,0,1:T(8,128)(2,1)} %all-gather.3.cloned.1.call-done), kind=kOutput, calls=%fused_computation.12 | convolution fusion | flops 7063339008 | bytes 28180480 | tf_op jit(solution)/shard_map/nf,df->nd/dot_general | solution.py:280
  239.1 0.5 broadcast_clamp_fusion.order_ref
  239.6 67.2 %all-to-all-done = bf16[16,2,384,512]{3,2,1,0:T(8,128)(2,1)} async-done(((bf16[16,2,384,512]{3,2,1,0:T(8,128)(2,1)}), bf16[16,2,384,512]{3,2,1,0:T(8,128)(2,1)}, u32[]{:S(2)}, u32[]{:S(2)}) %all-to-all-start) | async-done | bytes 12582944 | tf_op jit(solution)/shard_map/all_to_all | solution.py:241
  306.8 0.6 gather_fusion.5
  307.5 3.8 convolution_add_fusion.3
  311.3 0.7 gather_fusion.6
  312.6 0.7 reshape.382.q_ref
  313.6 0.7 pad_maximum_fusion.3.kv_ref
  314.2 17.0 %shard_map.148 = (bf16[16,384,512]{2,1,0:T(8,128)(2,1)}, bf16[16,2,6,128]{3,2,1,0:T(8,128)(2,1)}) custom-call(s32[16]{0:T(128)} %broadcast_clamp_fusion.order_ref, s32[16]{0:T(128)} %copy-done.8, bf16[32,384,512]{2,1,0:T(8,128)(2,1)} %bitcast.41.cache_ref, bf16[16,1,512]{2,1,0:T(2,128)(2,1)} %pad_maximum_fusion.3.kv_ref, bf16[16,2,6,128]{3,2,1,0:T(8,128)(2,1)} %reshape.382.q_ref), custom_call_target="tpu_custom_call" | custom-call | tf_op jit(solution)/shard_map/pallas_call | solution.py:121
  331.2 0.9 reshape.383
  332.2 3.2 multiply_reduce_fusion.1
  335.5 21.0 %all_to_all.25 = bf16[8,16,1536]{2,1,0:T(8,128)(2,1)S(1)} all-to-all(bf16[8,16,1536]{2,1,0:T(8,128)(2,1)S(1)} %broadcast_in_dim.66), channel_id=1, replica_groups=mesh['req'=16,'blk'=8] {'blk'}, dimensions={0} | all-to-all | bytes 786432 | tf_op jit(solution)/shard_map/all_to_all | solution.py:290
  356.5 4.9 %fusion.4 = f32[128,2,1120]{0,2,1:T(8,128)S(1)} fusion(bf16[128,1536,1]{1,0,2:T(8,128)(2,1)S(1)} %bitcast.185, bf16[1536,3,1120]{0,2,1:T(8,128)(2,1)} %copy.79), kind=kOutput, calls=%fused_computation.16 | convolution fusion | flops 880803840 | bytes 8421376 | tf_op jit(solution)/shard_map/nd,dkf->nkf/dot_general | solution.py:291
  361.4 3.4 fusion.17
  364.8 12.1 %all_to_all.26 = bf16[8,16,1536]{2,1,0:T(8,128)(2,1)S(1)} all-to-all(bf16[8,16,1536]{2,1,0:T(8,128)(2,1)S(1)} %bitcast.186), channel_id=1, replica_groups=mesh['req'=16,'blk'=8] {'blk'}, dimensions={0} | all-to-all | bytes 786432 | tf_op jit(solution)/shard_map/all_to_all | solution.py:301
  377.0 0.6 fusion.39
  377.6 2.2 fusion.26
  (94 shorter events, 3.2 us)
Async XLA Ops:
  7.2 76.2 %copy-start = (bf16[1,1,16,1536]{3,2,1,0:T(8,128)(2,1)S(1)}, bf16[1,1,16,1536]{3,2,1,0:T(8,128)(2,1)}, u32[]{:S(2)}) copy-start(bf16[1,1,16,1536]{3,2,1,0:T(8,128)(2,1)} %param.14) | copy-start | bytes 147460
  7.2 68.3 %all-gather.3.cloned.1.call-start = ((), (), s32[]{:S(2)}) async-start(), calls=%async_computation.6 | async-start | bytes 11280384 | tf_op jit(solution)/shard_map/all_gather | solution.py:191
  10.2 193.1 %all-gather.5.cloned.1.call-start = ((), (), s32[]{:S(2)}) async-start(), calls=%async_computation.7 | async-start | bytes 7077888 | tf_op jit(solution)/shard_map/all_gather | solution.py:275
  13.0 6.3 %copy-start.9 = (s32[1,1,17]{2,1,0:T(1,128)S(1)}, s32[1,1,17]{2,1,0:T(1,128)}, u32[]{:S(2)}) copy-start(s32[1,1,17]{2,1,0:T(1,128)} %param.17) | copy-start | bytes 208
  13.0 8.8 %copy-start.6 = (s32[1,1,17,24]{3,1,2,0:T(1,128)S(1)}, s32[1,1,17,24]{3,1,2,0:T(1,128)}, u32[]{:S(2)}) copy-start(s32[1,1,17,24]{3,1,2,0:T(1,128)} %param.16) | copy-start | bytes 4900
  17.9 1.3 copy-start.2
  19.2 9.0 %slice-start.2 = ((f32[256,2048]{1,0:T(8,128)}), f32[256,1536]{1,0:T(8,128)S(1)}, s32[]{:S(2)}) async-start(f32[256,2048]{1,0:T(8,128)} %copy-done.2), calls=%async_computation.11 | async-start | bytes 3145728 | tf_op jit(solution)/shard_map/slice | solution.py:44
  20.8 0.7 copy-start.4
  20.8 1.0 copy-start.5
  39.9 22.7 %copy-start.7 = (bf16[1536]{0:T(1024)(128)(2,1)S(1)}, bf16[1536]{0:T(1024)(128)(2,1)}, u32[]{:S(2)}) copy-start(bf16[1536]{0:T(1024)(128)(2,1)} %param.23) | copy-start | bytes 9220
  64.8 4.2 %slice-start = ((s8[4718592]{0:T(1024)(128)(4,1)}), s8[524288]{0:T(1024)(128)(4,1)S(1)}, s32[]{:S(2)}) async-start(s8[4718592]{0:T(1024)(128)(4,1)} %bitcast.168), calls=%async_computation.9 | async-start | bytes 1048576
  66.4 2.6 slice-start.1
  66.4 2.6 copy-start.3
  69.0 7.8 %copy-start.10 = (s32[1,1,17]{2,1,0:T(1,128)S(1)}, s32[1,1,17]{2,1,0:T(1,128)}, u32[]{:S(2)}) copy-start(s32[1,1,17]{2,1,0:T(1,128)} %param.17) | copy-start | bytes 208
  78.3 11.2 %all-to-all-start.2 = ((s32[16,2,128]{2,1,0:T(2,128)}), s32[16,2,128]{2,1,0:T(2,128)S(1)}, u32[]{:S(2)}, u32[]{:S(2)}) async-start(s32[16,2,128]{2,1,0:T(2,128)} %broadcast_in_dim.63), calls=%async_computation.3 | async-start | bytes 32768 | tf_op jit(solution)/shard_map/all_to_all | solution.py:210
  89.5 17.8 %all-to-all-start.1 = ((bf16[16,2,1536]{2,1,0:T(2,128)(2,1)}), bf16[16,2,1536]{2,1,0:T(2,128)(2,1)S(1)}, u32[]{:S(2)}, u32[]{:S(2)}) async-start(bf16[16,2,1536]{2,1,0:T(2,128)(2,1)} %reshape.376), calls=%async_computation.2 | async-start | bytes 196608 | tf_op jit(solution)/shard_map/all_to_all | solution.py:209
  107.3 199.5 %all-to-all-start = ((bf16[16,2,384,512]{3,2,1,0:T(8,128)(2,1)}), bf16[16,2,384,512]{3,2,1,0:T(8,128)(2,1)}, u32[]{:S(2)}, u32[]{:S(2)}) async-start(bf16[16,2,384,512]{3,2,1,0:T(8,128)(2,1)} %bitcast.167), calls=%async_computation.1 | async-start | bytes 25165824 | tf_op jit(solution)/shard_map/all_to_all | solution.py:241
  113.0 264.7 %reduce-scatter.2.cloned.1.call-start = ((), (), s32[]{:S(2)}) async-start(), calls=%async_computation.8 | async-start | bytes 7077888 | tf_op jit(solution)/shard_map/reduce_scatter | solution.py:309
  312.0 2.2 copy-start.8
  356.5 23.4 %copy-start.1 = (bf16[1,1,16,1536]{3,2,1,0:T(8,128)(2,1)S(1)}, bf16[1,1,16,1536]{3,2,1,0:T(8,128)(2,1)}, u32[]{:S(2)}) copy-start(bf16[1,1,16,1536]{3,2,1,0:T(8,128)(2,1)} %param.14) | copy-start | bytes 147460
Sparse Core Ops, SparseCore 0:
  10.3 65.1 all-gather.2
  78.4 124.8 all-gather.4
  238.9 125.0 reduce-scatter.1

commit v2 on v1

--- a/solution.py
+++ b/solution.py
@@ -11,6 +11,7 @@
 KEY_VALUE_HEADS = 2
 HEAD_SIZE = 128
 CAP = 2
+REQ = ("zx", "core")
 
 
 rms_eps = 1e-06
@@ -176,8 +177,8 @@
     gate_up,
     down_weight,
 ):
-    n_req = lax.axis_size("req")
-    own_index = lax.axis_index("req")
+    n_req = lax.axis_size(REQ)
+    own_index = lax.axis_index(REQ)
     slot_total = destination.shape[2]
     pool_rows = cache_pool[0, 0]
     table_rows = page_table[0, 0]
@@ -188,9 +189,9 @@
     slot_ids = jnp.arange(slot_total, dtype=jnp.int32)
 
     local_down = jnp.transpose(down_weight)[:, None, :]
-    all_weights = lax.all_gather(
-        jnp.concatenate([gate_up, local_down], axis=1), "req", axis=0, tiled=True
-    )
+    chip_weights = lax.all_gather(jnp.concatenate([gate_up, local_down], axis=1), "zx", axis=0)
+    all_weights = lax.all_gather(chip_weights, "core", axis=1)
+    all_weights = all_weights.reshape((-1,) + all_weights.shape[3:])
 
     send_dest = destination[0, 0]
     decode_x = decode_rows[0, 0]
@@ -206,8 +207,8 @@
     send_cache = pool_rows[send_pages].reshape(n_req, CAP, cache_length, width_per_row)
     send_x = decode_x[picked].reshape(n_req, CAP, -1)
     send_len = jnp.broadcast_to(own_len[picked].reshape(n_req, CAP, 1), (n_req, CAP, 128))
-    recv_x = lax.all_to_all(send_x, "req", split_axis=0, concat_axis=0, tiled=True)
-    recv_len = lax.all_to_all(send_len, "req", split_axis=0, concat_axis=0, tiled=True)
+    recv_x = lax.all_to_all(send_x, REQ, split_axis=0, concat_axis=0, tiled=True)
+    recv_len = lax.all_to_all(send_len, REQ, split_axis=0, concat_axis=0, tiled=True)
 
     shift = jnp.mod(send_dest - own_index, n_req)
     source = jnp.mod(own_index - shift, n_req)
@@ -238,7 +239,7 @@
     all_weights, prefill_res, send_cache = lax.optimization_barrier(
         (all_weights, prefill_res, send_cache)
     )
-    recv_cache = lax.all_to_all(send_cache, "req", split_axis=0, concat_axis=0, tiled=True)
+    recv_cache = lax.all_to_all(send_cache, REQ, split_axis=0, concat_axis=0, tiled=True)
     prefill_partial = feed_forward_partial(prefill_res, mlp_gain, all_weights)
     _, recv_cache, recv_x, recv_len = lax.optimization_barrier(
         (prefill_partial, recv_cache, recv_x, recv_len)
@@ -311,28 +312,32 @@
 
 
 def solution(mesh):
+    req_size = mesh.shape["req"]
+    split_mesh = jax.sharding.Mesh(
+        mesh.devices.reshape(req_size // 2, 2, mesh.shape["blk"]), ("zx", "core", "blk")
+    )
     return jax.shard_map(
         shards,
-        mesh=mesh,
+        mesh=split_mesh,
         in_specs=(
-            P("blk", "req", None, None),
-            P("blk", "req", None, None),
-            P("blk", "req", None, None, None),
-            P("blk", "req", None, None),
-            P("blk", "req", None),
-            P("blk", "req", None),
-            P(),
-            P(),
-            P(),
-            P(),
-            P(),
-            P("req", None, "blk"),
-            P("blk", "req"),
+            P("blk", REQ, None, None),
+            P("blk", REQ, None, None),
+            P("blk", REQ, None, None, None),
+            P("blk", REQ, None, None),
+            P("blk", REQ, None),
+            P("blk", REQ, None),
+            P(),
+            P(),
+            P(),
+            P(),
+            P(),
+            P(REQ, None, "blk"),
+            P("blk", REQ),
         ),
         out_specs=(
-            P("blk", "req", None, None),
-            P("blk", "req", None, None),
-            P("blk", "req", None, None, None),
+            P("blk", REQ, None, None),
+            P("blk", REQ, None, None),
+            P("blk", REQ, None, None, None),
         ),
         check_vma=False,
     )

time: 388 us -> 511 us (1.32)
  waiting for transfers between devices: 167 us -> 278 us
  local copies, waits for them, and re-layouts: 57.1 us -> 72.3 us
    all_gather x1 -> x2, waiting for transfers between devices: 5.06 us -> 114 us  [the longest x1 114 us: shards(): lax.all_gather(jnp.concatenate([gate_up, local_down], axis=1), 'zx', axis=0)]
    mul x6, local copies, waits for them, and re-layouts: 3.25 us -> 8.45 us  [apply_rotary(): return vectors * cosine + turned * sine_table]
  transfers between devices with their start and end apart: 6 -> 7, of which waited for: 4 -> 4; matrix products, arithmetic and copies ran while one was open for 34% -> 29% of each run, Pallas kernels for 4% -> 3%
where the time goes in v2:
time: 511 us; the launch traced here: 509 us
  waiting for transfers between devices  278 us (54%)
  local copies, waits for them, and re-layouts  72.3 us (14%)
  matrix products  60.6 us (12%)
  blocking collectives  32.5 us (6%)
  other arithmetic  21.2 us (4%)
  Pallas kernels  17 us (3%)
  between operations  14.4 us (3%)
  starting transfers between devices  13.4 us (3%)
    all_gather x1, waiting for transfers between devices, shards(): lax.all_gather(jnp.concatenate([gate_up, local_down], axis=1), 'zx', axis=0)  114 us
    all_gather x1, waiting for transfers between devices, feed_forward_partial(): lax.all_gather(mlp_in, 'blk', axis=0, tiled=True)  88.7 us
    all_to_all x1, waiting for transfers between devices, shards(): lax.all_to_all(send_cache, REQ, split_axis=0, concat_axis=0, tiled=True)  70.1 us
    gather x1, local copies, waits for them, and re-layouts, shards(): pool_rows[send_pages].reshape(n_req, CAP, cache_length, width_per_row)  22.6 us
    dot_general x1, matrix products, feed_forward_partial(): jnp.einsum('nd,dkf->nkf', lax.all_gather(mlp_in, 'blk', axis=0, tiled=Tru...  20.5 us
    all_to_all x1, blocking collectives, small_feed_forward(): lax.all_to_all(spread, 'blk', split_axis=0, concat_axis=0, tiled=True)  19.9 us
    pallas_call x1, Pallas kernels, decode_attend(): pl.pallas_call(decode_kernel, grid_spec=pltpu.PrefetchScalarGridSpec(num_...  17 us
    dot_general x1, matrix products, feed_forward_partial(): jnp.einsum('nf,df->nd', hidden, all_weights[:, 2, :], preferred_element_t...  15 us
  transfers between devices with their start and end apart: 7, of which 4 were waited for; matrix products, arithmetic and copies ran while one was open for 29% of the time, Pallas kernels for 3%

profile of v2, /device:TPU:0, one launch (start us, length us, event | category | flops | bytes accessed | tf_op | source)
XLA Modules:
  0.0 509.1 jit_solution(16202781470285041117)
XLA Ops:
  7.3 1.1 copy.69
  8.4 1.9 pad_maximum_fusion
  10.3 114.0 %all-gather.8.cloned.1.call-done = bf16[768,3,1120]{2,0,1:T(8,128)(2,1)} async-done(((bf16[96,3,1120]{2,0,1:T(8,128)(2,1)}), bf16[768,3,1120]{2,0,1:T(8,128)(2,1)}) %all-gather.8.cloned.1.call-update) | async-done | bytes 5160976 | tf_op jit(solution)/shard_map/all_gather | solution.py:192
  124.7 4.6 convolution_add_fusion.1
  129.4 0.7 slice.119
  130.1 1.3 slice.125
  131.4 0.6 slice.82
  132.0 0.7 add_convert_fusion.3
  133.0 0.6 copy-done.3
  133.7 0.7 copy.71
  134.4 1.1 reshape.373
  135.5 0.7 copy.70
  136.3 5.8 %gather_fusion = bf16[24,16,512]{2,1,0:T(8,128)(2,1)} fusion(bf16[408,16,512]{2,1,0:T(8,128)(2,1)} %bitcast.172, s32[1024]{0:T(1024)S(1)} %pad_clamp_fusion.4), kind=kCustom, calls=%fused_computation | custom fusion | bytes 786528 | tf_op jit(solution)/shard_map/gather | solution.py:187
  142.1 0.3 slice_negate_fusion.1
  142.5 1.3 maximum_multiply_fusion.1
  143.8 1.1 mul.267
  144.9 1.2 maximum_bitcast_fusion
  146.1 0.9 fusion.58
  146.9 1.2 copy.73
  148.1 3.1 copy.75
  151.2 1.5 slice_negate_fusion
  152.7 1.3 maximum_multiply_fusion
  154.0 3.1 copy.76
  157.1 1.3 mul.273
  158.3 3.0 copy.74
  161.4 3.1 add_convert_fusion.1
  164.4 1.4 copy.77
  165.8 1.2 copy.72
  167.4 0.6 gather_fusion.1
  168.1 22.6 %gather_fusion.2 = bf16[768,16,512]{2,1,0:T(8,128)(2,1)} fusion(bf16[408,16,512]{2,1,0:T(8,128)(2,1)} %bitcast.173, s32[1024]{0:T(1024)S(1)} %pad_clamp_fusion.2), kind=kCustom, calls=%fused_computation.2 | custom fusion | bytes 25168896 | tf_op jit(solution)/shard_map/gather | solution.py:207
  190.7 0.7 iota_compare_fusion.4
  191.5 1.3 fusion.7
  192.9 1.6 fusion.1
  194.5 2.5 fusion.23
  197.0 1.4 convolution_add_fusion
  198.7 1.1 multiply_convert_fusion
  199.8 0.7 gather_fusion.4
  200.6 0.7 broadcast_in_dim.63
  201.3 4.0 all-to-all-start.2
  205.3 0.6 gather_fusion.3
  206.0 0.7 reshape.380
  206.7 4.7 all-to-all-done.2
  211.4 3.5 all-to-all-start.1
  214.9 14.2 %copy.81 = bf16[1536,3,1120]{0,2,1:T(8,128)(2,1)} copy(bf16[1536,3,1120]{2,0,1:T(8,128)(2,1)} %bitcast.175) | data formatting | bytes 20643840 | tf_op jit(solution)/shard_map/optimization_barrier | solution.py:239
  229.2 5.7 %all-to-all-start = ((bf16[16,2,384,512]{3,2,1,0:T(8,128)(2,1)}), bf16[16,2,384,512]{3,2,1,0:T(8,128)(2,1)}, u32[]{:S(2)}, u32[]{:S(2)}) async-start(bf16[16,2,384,512]{3,2,1,0:T(8,128)(2,1)} %bitcast.169), calls=%async_computation.1 | async-start | bytes 25165824 | tf_op jit(solution)/shard_map/all_to_all | solution.py:242
  234.9 88.7 %all-gather.6.cloned.1.call-done = bf16[2048,1536]{1,0:T(8,128)(2,1)} async-done(((bf16[256,1536]{1,0:T(8,128)(2,1)}), bf16[2048,1536]{1,0:T(8,128)(2,1)}) %all-gather.6.cloned.1.call-update) | async-done | bytes 6291472 | tf_op jit(solution)/shard_map/all_gather | solution.py:276
  323.7 20.5 %fusion.2 = f32[2048,2,1120]{0,2,1:T(8,128)} fusion(bf16[2048,1536]{1,0:T(8,128)(2,1)} %all-gather.6.cloned.1.call-done, bf16[1536,3,1120]{0,2,1:T(8,128)(2,1)} %copy.81), kind=kOutput, calls=%fused_computation.14 | convolution fusion | flops 14092861440 | bytes 31522816 | tf_op jit(solution)/shard_map/nd,dkf->nkf/dot_general | solution.py:274
  344.2 15.0 %convolution_convert_fusion = bf16[2048,1536]{1,0:T(8,128)(2,1)} fusion(f32[2048,2,1120]{0,2,1:T(8,128)} %fusion.2, bf16[1536,3,1120]{2,0,1:T(8,128)(2,1)} %bitcast.176), kind=kOutput, calls=%fused_computation.12 | convolution fusion | flops 7063339008 | bytes 28180480 | tf_op jit(solution)/shard_map/nf,df->nd/dot_general | solution.py:281
  359.5 0.6 broadcast_clamp_fusion.order_ref
  360.1 70.1 %all-to-all-done = bf16[16,2,384,512]{3,2,1,0:T(8,128)(2,1)} async-done(((bf16[16,2,384,512]{3,2,1,0:T(8,128)(2,1)}), bf16[16,2,384,512]{3,2,1,0:T(8,128)(2,1)}, u32[]{:S(2)}, u32[]{:S(2)}) %all-to-all-start) | async-done | bytes 12582944 | tf_op jit(solution)/shard_map/all_to_all | solution.py:242
  430.2 0.6 gather_fusion.5
  430.9 3.8 convolution_add_fusion.3
  434.7 0.7 gather_fusion.6
  436.0 0.7 reshape.386.q_ref
  437.0 0.7 pad_maximum_fusion.3.kv_ref
  437.6 17.0 %shard_map.148 = (bf16[16,384,512]{2,1,0:T(8,128)(2,1)}, bf16[16,2,6,128]{3,2,1,0:T(8,128)(2,1)}) custom-call(s32[16]{0:T(128)} %broadcast_clamp_fusion.order_ref, s32[16]{0:T(128)} %copy-done.11, bf16[32,384,512]{2,1,0:T(8,128)(2,1)} %bitcast.43.cache_ref, bf16[16,1,512]{2,1,0:T(2,128)(2,1)} %pad_maximum_fusion.3.kv_ref, bf16[16,2,6,128]{3,2,1,0:T(8,128)(2,1)} %reshape.386.q_ref), custom_call_target="tpu_custom_call" | custom-call | tf_op jit(solution)/shard_map/pallas_call | solution.py:122
  454.6 0.9 reshape.387
  455.6 3.2 multiply_reduce_fusion.1
  458.9 19.9 %all_to_all.25 = bf16[8,16,1536]{2,1,0:T(8,128)(2,1)S(1)} all-to-all(bf16[8,16,1536]{2,1,0:T(8,128)(2,1)S(1)} %broadcast_in_dim.66), channel_id=1, replica_groups=mesh['zx'=8,'core'=2,'blk'=8] {'blk'}, dimensions={0} | all-to-all | bytes 786432 | tf_op jit(solution)/shard_map/all_to_all | solution.py:291
  478.8 5.0 fusion.4
  483.8 3.4 fusion.17
  487.1 12.5 %all_to_all.26 = bf16[8,16,1536]{2,1,0:T(8,128)(2,1)S(1)} all-to-all(bf16[8,16,1536]{2,1,0:T(8,128)(2,1)S(1)} %bitcast.192), channel_id=1, replica_groups=mesh['zx'=8,'core'=2,'blk'=8] {'blk'}, dimensions={0} | all-to-all | bytes 786432 | tf_op jit(solution)/shard_map/all_to_all | solution.py:302
  499.7 0.6 fusion.39
  500.4 2.2 fusion.26
  (104 shorter events, 3.4 us)
Async XLA Ops:
  7.2 198.2 %copy-start = (bf16[1,1,16,1536]{3,2,1,0:T(8,128)(2,1)S(1)}, bf16[1,1,16,1536]{3,2,1,0:T(8,128)(2,1)}, u32[]{:S(2)}) copy-start(bf16[1,1,16,1536]{3,2,1,0:T(8,128)(2,1)} %param.14) | copy-start | bytes 147460
  7.2 117.2 %copy-start.8 = (bf16[1536]{0:T(1024)(128)(2,1)S(1)}, bf16[1536]{0:T(1024)(128)(2,1)}, u32[]{:S(2)}) copy-start(bf16[1536]{0:T(1024)(128)(2,1)} %param.19) | copy-start | bytes 9220
  7.2 117.2 %copy-start.9 = (bf16[2048]{0:T(1024)(128)(2,1)S(1)}, bf16[2048]{0:T(1024)(128)(2,1)}, u32[]{:S(2)}) copy-start(bf16[2048]{0:T(1024)(128)(2,1)} %param.21) | copy-start | bytes 12292
  7.2 117.3 %copy-start.2 = (bf16[1,1,256,1536]{3,2,1,0:T(8,128)(2,1)S(1)}, bf16[1,1,256,1536]{3,2,1,0:T(8,128)(2,1)}, u32[]{:S(2)}) copy-start(bf16[1,1,256,1536]{3,2,1,0:T(8,128)(2,1)} %param.13) | copy-start | bytes 2359300
  7.2 117.1 %all-gather.8.cloned.1.call-start = ((), (), s32[]{:S(2)}) async-start(), calls=%async_computation.8 | async-start | bytes 5971968 | tf_op jit(solution)/shard_map/all_gather | solution.py:192
  10.3 188.2 %all-gather.10.cloned.1.call-start = ((), (), s32[]{:S(2)}) async-start(), calls=%async_computation.9 | async-start | bytes 15925248 | tf_op jit(solution)/shard_map/all_gather | solution.py:193
  124.4 199.3 %all-gather.6.cloned.1.call-start = ((), (), s32[]{:S(2)}) async-start(), calls=%async_computation.6 | async-start | bytes 7077888 | tf_op jit(solution)/shard_map/all_gather | solution.py:276
  124.7 6.7 %copy-start.13 = (s32[1,1,17]{2,1,0:T(1,128)S(1)}, s32[1,1,17]{2,1,0:T(1,128)}, u32[]{:S(2)}) copy-start(s32[1,1,17]{2,1,0:T(1,128)} %param.17) | copy-start | bytes 208
  124.7 11.6 %copy-start.7 = (s32[1,1,17,24]{3,1,2,0:T(1,128)S(1)}, s32[1,1,17,24]{3,1,2,0:T(1,128)}, u32[]{:S(2)}) copy-start(s32[1,1,17,24]{3,1,2,0:T(1,128)} %param.16) | copy-start | bytes 4900
  133.0 0.6 copy-start.3
  133.0 2.5 copy-start.5
  142.5 10.3 %copy-start.4 = (f32[256,128]{0,1:T(8,128)S(1)}, f32[256,128]{0,1:T(8,128)}, u32[]{:S(2)}) copy-start(f32[256,128]{0,1:T(8,128)} %copy-done.3) | copy-start | bytes 393220
  148.1 8.9 %copy-start.6 = (f32[256,128]{0,1:T(8,128)S(1)}, f32[256,128]{0,1:T(8,128)}, u32[]{:S(2)}) copy-start(f32[256,128]{0,1:T(8,128)} %copy-done.5) | copy-start | bytes 393220
  157.1 10.0 %copy-start.12 = (s32[1,1,16]{2,1,0:T(1,128)S(1)}, s32[1,1,16]{2,1,0:T(1,128)}, u32[]{:S(2)}) copy-start(s32[1,1,16]{2,1,0:T(1,128)} %param.18) | copy-start | bytes 196
  168.0 22.6 %copy-start.10 = (bf16[1536]{0:T(1024)(128)(2,1)S(1)}, bf16[1536]{0:T(1024)(128)(2,1)}, u32[]{:S(2)}) copy-start(bf16[1536]{0:T(1024)(128)(2,1)} %param.23) | copy-start | bytes 9220
  192.9 4.1 slice-start
  194.5 2.5 slice-start.1
  197.0 2.8 copy-start.14
  201.3 10.1 %all-to-all-start.2 = ((s32[16,2,128]{2,1,0:T(2,128)}), s32[16,2,128]{2,1,0:T(2,128)S(1)}, u32[]{:S(2)}, u32[]{:S(2)}) async-start(s32[16,2,128]{2,1,0:T(2,128)} %broadcast_in_dim.63), calls=%async_computation.3 | async-start | bytes 32768 | tf_op jit(solution)/shard_map/all_to_all | solution.py:211
  211.4 17.8 %all-to-all-start.1 = ((bf16[16,2,1536]{2,1,0:T(2,128)(2,1)}), bf16[16,2,1536]{2,1,0:T(2,128)(2,1)S(1)}, u32[]{:S(2)}, u32[]{:S(2)}) async-start(bf16[16,2,1536]{2,1,0:T(2,128)(2,1)} %reshape.380), calls=%async_computation.2 | async-start | bytes 196608 | tf_op jit(solution)/shard_map/all_to_all | solution.py:210
  229.2 201.0 %all-to-all-start = ((bf16[16,2,384,512]{3,2,1,0:T(8,128)(2,1)}), bf16[16,2,384,512]{3,2,1,0:T(8,128)(2,1)}, u32[]{:S(2)}, u32[]{:S(2)}) async-start(bf16[16,2,384,512]{3,2,1,0:T(8,128)(2,1)} %bitcast.169), calls=%async_computation.1 | async-start | bytes 25165824 | tf_op jit(solution)/shard_map/all_to_all | solution.py:242
  234.9 265.5 %reduce-scatter.2.cloned.1.call-start = ((), (), s32[]{:S(2)}) async-start(), calls=%async_computation.7 | async-start | bytes 7077888 | tf_op jit(solution)/shard_map/reduce_scatter | solution.py:310
  435.4 2.2 copy-start.11
  478.8 23.8 %copy-start.1 = (bf16[1,1,16,1536]{3,2,1,0:T(8,128)(2,1)S(1)}, bf16[1,1,16,1536]{3,2,1,0:T(8,128)(2,1)}, u32[]{:S(2)}) copy-start(bf16[1,1,16,1536]{3,2,1,0:T(8,128)(2,1)} %param.14) | copy-start | bytes 147460
Sparse Core Ops, SparseCore 0:
  10.4 113.9 all-gather.7
  126.0 25.5 all-gather.9
  199.9 123.7 all-gather.5
  359.3 125.5 reduce-scatter.1

commit v3 on v1

--- a/solution.py
+++ b/solution.py
@@ -113,9 +113,9 @@
         )
 
 
-def decode_attend(arrival_order, got_length, recv_cache, decode_kv, decode_q):
+def decode_attend(arrival_order, got_length, recv_cache, decode_kv, decode_q, cache_length):
     count = arrival_order.shape[0]
-    cache_length, width_per_row = recv_cache.shape[1:]
+    width_per_row = recv_cache.shape[2]
     group_width = QUERY_HEADS // KEY_VALUE_HEADS
     order = jnp.clip(arrival_order, 0, recv_cache.shape[0] - 1)
     new_cache, attended = pl.pallas_call(
@@ -203,11 +203,22 @@
     matches = target[None, :] == flat_slots[:, None]
     picked = jnp.sum(jnp.where(matches, slot_ids[None, :], 0), axis=1)
     send_pages = table_rows[picked]
-    send_cache = pool_rows[send_pages].reshape(n_req, CAP, cache_length, width_per_row)
-    send_x = decode_x[picked].reshape(n_req, CAP, -1)
-    send_len = jnp.broadcast_to(own_len[picked].reshape(n_req, CAP, 1), (n_req, CAP, 128))
-    recv_x = lax.all_to_all(send_x, "req", split_axis=0, concat_axis=0, tiled=True)
-    recv_len = lax.all_to_all(send_len, "req", split_axis=0, concat_axis=0, tiled=True)
+    send_count = n_req * CAP
+    row_parts = decode_x.shape[1] // width_per_row
+    sent_len = own_len[picked]
+    length_code = jnp.stack([sent_len // 16, sent_len % 16], axis=1).astype(jnp.bfloat16)
+    extra_rows = jnp.concatenate(
+        [
+            decode_x[picked].reshape(send_count, row_parts, width_per_row),
+            jnp.pad(length_code, ((0, 0), (0, width_per_row - 2)))[:, None, :],
+            jnp.zeros((send_count, 8 - row_parts - 1, width_per_row), jnp.bfloat16),
+        ],
+        axis=1,
+    )
+    send_cache = jnp.concatenate(
+        [pool_rows[send_pages].reshape(send_count, cache_length, width_per_row), extra_rows],
+        axis=1,
+    ).reshape(n_req, CAP, cache_length + 8, width_per_row)
 
     shift = jnp.mod(send_dest - own_index, n_req)
     source = jnp.mod(own_index - shift, n_req)
@@ -240,12 +251,13 @@
     )
     recv_cache = lax.all_to_all(send_cache, "req", split_axis=0, concat_axis=0, tiled=True)
     prefill_partial = feed_forward_partial(prefill_res, mlp_gain, all_weights)
-    _, recv_cache, recv_x, recv_len = lax.optimization_barrier(
-        (prefill_partial, recv_cache, recv_x, recv_len)
-    )
+    _, recv_cache = lax.optimization_barrier((prefill_partial, recv_cache))
     prefill_out = feed_forward_finish(prefill_res, prefill_partial)
-    got_x = recv_x.reshape(n_req * CAP, -1)[arrival_order]
-    got_length = recv_len.reshape(n_req * CAP, 128)[arrival_order, 0]
+    recv_cache = recv_cache.reshape(n_req * CAP, cache_length + 8, width_per_row)
+    got_extra = recv_cache[arrival_order, cache_length:, :]
+    got_x = got_extra[:, :row_parts, :].reshape(slot_total, -1)
+    got_code = got_extra[:, row_parts, :2].astype(jnp.int32)
+    got_length = got_code[:, 0] * 16 + got_code[:, 1]
 
     decode_q, decode_kv = project(
         rms_scale(got_x, attn_gain), inproj_weight, inproj_bias, got_length
@@ -253,9 +265,10 @@
     cache_after, decode_att = decode_attend(
         arrival_order,
         got_length,
-        recv_cache.reshape(n_req * CAP, cache_length, width_per_row),
+        recv_cache,
         decode_kv,
         decode_q,
+        cache_length,
     )
     decode_res = got_x.astype(jnp.float32) + jnp.dot(
         decode_att, outproj_weight, preferred_element_type=jnp.float32

time: 388 us -> 410 us (1.057); the launches traced: 386 us -> 403 us
  local copies, waits for them, and re-layouts: 57.1 us -> 94.3 us
  waiting for transfers between devices: 167 us -> 142 us
  other arithmetic: 22.2 us -> 36.9 us
  starting transfers between devices: 14.4 us -> 6.48 us
    all_to_all x1, waiting for transfers between devices: 67.2 us -> 29 us  [shards(): lax.all_to_all(send_cache, 'req', split_axis=0, concat_axis=0, tiled=True)]
    reshape x2 -> x1, local copies, waits for them, and re-layouts: 0.72 us -> 29.5 us  [shards(): recv_cache.reshape(n_req * CAP, cache_length + 8, width_per_row)]
    all_gather x1, waiting for transfers between devices: 90.2 us -> 113 us  [feed_forward_partial(): lax.all_gather(mlp_in, 'blk', axis=0, tiled=True)]
    concatenate x0 -> x2, other arithmetic: none -> 14.3 us  [the longest x1 14.3 us: shards(): jnp.concatenate([pool_rows[send_pages].reshape(send_count, cache_length,...]
    all_to_all x2 -> x0, starting transfers between devices: 8.58 us -> none  [the longest x1 5.08 us: shards(): lax.all_to_all(send_len, 'req', split_axis=0, concat_axis=0, tiled=True)]
    all_gather x1, waiting for transfers between devices: 5.06 us -> 0.01 us  [shards(): lax.all_gather(jnp.concatenate([gate_up, local_down], axis=1), 'req', axi...]
    all_to_all x2 -> x0, waiting for transfers between devices: 4.74 us -> none  [the longest x1 4.74 us: shards(): lax.all_to_all(send_len, 'req', split_axis=0, concat_axis=0, tiled=True)]
    mul x6, local copies, waits for them, and re-layouts: 3.25 us -> 7.49 us  [apply_rotary(): return vectors * cosine + turned * sine_table]
  transfers between devices with their start and end apart: 6 -> 4, of which waited for: 4 -> 2; matrix products, arithmetic and copies ran while one was open for 34% -> 46% of each run, Pallas kernels for 4% -> 4%
where the time goes in v3:
time: 410 us; the launch traced here: 403 us
  waiting for transfers between devices  142 us (35%)
  local copies, waits for them, and re-layouts  94.3 us (23%)
  matrix products  61 us (15%)
  other arithmetic  36.9 us (9%)
  blocking collectives  30.6 us (7%)
  Pallas kernels  17.1 us (4%)
  between operations  14.6 us (4%)
  starting transfers between devices  6.48 us (2%)
    all_gather x1, waiting for transfers between devices, feed_forward_partial(): lax.all_gather(mlp_in, 'blk', axis=0, tiled=True)  113 us
    reshape x1, local copies, waits for them, and re-layouts, shards(): recv_cache.reshape(n_req * CAP, cache_length + 8, width_per_row)  29.5 us
    all_to_all x1, waiting for transfers between devices, shards(): lax.all_to_all(send_cache, 'req', split_axis=0, concat_axis=0, tiled=True)  29 us
    gather x1, local copies, waits for them, and re-layouts, shards(): pool_rows[send_pages].reshape(send_count, cache_length, width_per_row)  22.9 us
    dot_general x1, matrix products, feed_forward_partial(): jnp.einsum('nd,dkf->nkf', lax.all_gather(mlp_in, 'blk', axis=0, tiled=Tru...  20.5 us
    pallas_call x1, Pallas kernels, decode_attend(): pl.pallas_call(decode_kernel, grid_spec=pltpu.PrefetchScalarGridSpec(num_...  17.1 us
    all_to_all x1, blocking collectives, small_feed_forward(): lax.all_to_all(spread, 'blk', split_axis=0, concat_axis=0, tiled=True)  16.9 us
    dot_general x1, matrix products, feed_forward_partial(): jnp.einsum('nf,df->nd', hidden, all_weights[:, 2, :], preferred_element_t...  15.1 us
  transfers between devices with their start and end apart: 4, of which 2 were waited for; matrix products, arithmetic and copies ran while one was open for 46% of the time, Pallas kernels for 4%

profile of v3, /device:TPU:0, one launch (start us, length us, event | category | flops | bytes accessed | tf_op | source)
XLA Modules:
  0.0 403.0 jit_solution(2763934975687248130)
XLA Ops:
  7.2 1.1 copy.106
  8.3 1.9 pad_maximum_fusion
  10.2 0.7 convert_element_type.134
  10.9 0.7 convert_element_type.136
  11.6 1.4 fusion.20
  13.0 4.9 %convolution_add_fusion.1 = f32[256,2048]{1,0:T(8,128)S(1)} fusion(bf16[1536,2048]{1,0:T(8,128)(2,1)} %param.20, f32[2048]{0:T(1024)S(1)} %convert_element_type.136, bf16[1,1,256,1536]{3,2,1,0:T(8,128)(2,1)} %param.13, f32[1536]{0:T(1024)S(1)} %convert_element_type.134, f32[256]{0:T(256)S(1)} %add_rsqrt_fusion.1), kind=kOutput, calls=%fused_computation.29 | convolution fusion | flops 1612709888 | bytes 9190400 | tf_op jit(solution)/shard_map/dot_general | solution.py:38
  18.0 1.3 slice.139
  19.3 0.6 slice.94
  19.9 0.2 convert_reduce_fusion.2
  20.1 0.6 iota_add_fusion
  20.6 0.5 multiply_add_fusion
  21.3 0.7 gather_fusion.4
  22.1 0.6 gather_fusion.1
  22.8 0.6 concatenate.91
  23.4 0.6 gather_fusion.3
  24.2 0.7 add_convert_fusion.3
  24.8 0.3 multiply_cosine_fusion
  25.4 1.3 mul.278
  26.7 3.1 copy.111
  29.9 3.7 gather_fusion
  33.6 0.3 slice_negate_fusion.1
  33.9 0.4 maximum_multiply_fusion.1
  34.5 0.2 copy.110
  34.7 0.9 copy.109
  35.7 3.1 copy.112
  38.7 1.6 slice_negate_fusion
  40.3 1.3 maximum_multiply_fusion
  41.5 3.0 copy.113
  44.6 2.3 add_convert_fusion.1
  46.9 0.3 copy.114
  47.1 22.9 %gather_fusion.2 = bf16[768,16,512]{2,1,0:T(8,128)(2,1)} fusion(bf16[408,16,512]{2,1,0:T(8,128)(2,1)} %bitcast.192, s32[1024]{0:T(1024)S(1)} %pad_clamp_fusion.1), kind=kCustom, calls=%fused_computation.2 | custom fusion | bytes 25168896 | tf_op jit(solution)/shard_map/gather | solution.py:219
  70.0 0.7 iota_compare_fusion.4
  71.0 1.3 fusion.7
  72.3 1.6 fusion.1
  74.0 2.5 fusion.23
  76.6 1.4 convolution_add_fusion
  78.0 1.1 slice-done.2
  79.1 14.3 %maximum_maximum_fusion = bf16[16,2,392,512]{3,2,1,0:T(8,128)(2,1)} fusion(bf16[16,2,1,512]{3,2,1,0:T(2,128)(2,1)S(1)} %copy-done.4, bf16[16,2,3,512]{3,2,1,0:T(4,128)(2,1)S(1)} %concatenate.78, bf16[16,2,384,512]{3,2,1,0:T(8,128)(2,1)S(1)} %bitcast.188, bf16[392]{0:T(512)(128)(2,1)S(1)} %pad.19.clone), kind=kLoop, calls=%fused_computation.6 | loop fusion | flops 51380224 | bytes 25559824 | tf_op jit(solution)/shard_map/concatenate | solution.py:218
  93.4 0.2 multiply_reduce_fusion
  93.6 1.1 multiply_convert_fusion
  94.7 6.4 %all-to-all-start = ((bf16[16,2,392,512]{3,2,1,0:T(8,128)(2,1)}), bf16[16,2,392,512]{3,2,1,0:T(8,128)(2,1)}, u32[]{:S(2)}, u32[]{:S(2)}) async-start(bf16[16,2,392,512]{3,2,1,0:T(8,128)(2,1)} %maximum_maximum_fusion), calls=%async_computation.1 | async-start | bytes 25690112 | tf_op jit(solution)/shard_map/all_to_all | solution.py:252
  101.1 14.6 %copy.120 = bf16[1536,3,1120]{0,2,1:T(8,128)(2,1)} copy(bf16[1536,3,1120]{2,0,1:T(8,128)(2,1)} %all-gather.3.cloned.1.call-done) | data formatting | bytes 20643840 | tf_op jit(solution)/shard_map/optimization_barrier | solution.py:249
  115.7 112.9 %all-gather.5.cloned.1.call-done = bf16[2048,1536]{1,0:T(8,128)(2,1)} async-done(((bf16[256,1536]{1,0:T(8,128)(2,1)}), bf16[2048,1536]{1,0:T(8,128)(2,1)}) %all-gather.5.cloned.1.call-update) | async-done | bytes 6291472 | tf_op jit(solution)/shard_map/all_gather | solution.py:288
  228.6 20.5 %fusion.2 = f32[2048,2,1120]{0,2,1:T(8,128)} fusion(bf16[2048,1536]{1,0:T(8,128)(2,1)} %all-gather.5.cloned.1.call-done, bf16[1536,3,1120]{0,2,1:T(8,128)(2,1)} %copy.120), kind=kOutput, calls=%fused_computation.14 | convolution fusion | flops 14092861440 | bytes 31522816 | tf_op jit(solution)/shard_map/nd,dkf->nkf/dot_general | solution.py:286
  249.1 15.1 %convolution_convert_fusion = bf16[2048,1536]{1,0:T(8,128)(2,1)} fusion(f32[2048,2,1120]{0,2,1:T(8,128)} %fusion.2, bf16[1536,3,1120]{2,0,1:T(8,128)(2,1)} %all-gather.3.cloned.1.call-done), kind=kOutput, calls=%fused_computation.12 | convolution fusion | flops 7063339008 | bytes 28180480 | tf_op jit(solution)/shard_map/nf,df->nd/dot_general | solution.py:293
  264.1 0.6 copy-done.9
  264.8 0.2 convert_reduce_fusion.1
  265.1 0.6 broadcast_clamp_fusion.order_ref
  265.7 29.0 %all-to-all-done = bf16[16,2,392,512]{3,2,1,0:T(8,128)(2,1)} async-done(((bf16[16,2,392,512]{3,2,1,0:T(8,128)(2,1)}), bf16[16,2,392,512]{3,2,1,0:T(8,128)(2,1)}, u32[]{:S(2)}, u32[]{:S(2)}) %all-to-all-start) | async-done | bytes 12845088 | tf_op jit(solution)/shard_map/all_to_all | solution.py:252
  294.7 29.5 %copy.121 = bf16[32,392,512]{2,0,1:T(8,128)(2,1)} copy(bf16[32,392,512]{2,1,0:T(8,128)(2,1)} %bitcast.38.cache_ref) | data formatting | bytes 25690112 | tf_op jit(solution)/shard_map/reshape | solution.py:256
  324.2 1.8 gather_fusion.5
  326.1 3.9 convolution_add_fusion.3
  330.2 0.6 convert_bitcast_fusion.1
  331.7 0.7 reshape.451.q_ref
  332.4 0.7 pad_maximum_fusion.3.kv_ref
  333.0 17.1 %shard_map.148 = (bf16[16,384,512]{2,1,0:T(8,128)(2,1)}, bf16[16,2,6,128]{3,2,1,0:T(8,128)(2,1)}) custom-call(s32[16]{0:T(128)} %broadcast_clamp_fusion.order_ref, s32[16]{0:T(128)} %bitcast.213, bf16[32,392,512]{2,1,0:T(8,128)(2,1)} %bitcast.38.cache_ref, bf16[16,1,512]{2,1,0:T(2,128)(2,1)} %pad_maximum_fusion.3.kv_ref, bf16[16,2,6,128]{3,2,1,0:T(8,128)(2,1)} %reshape.451.q_ref), custom_call_target="tpu_custom_call" | custom-call | tf_op jit(solution)/shard_map/pallas_call | solution.py:121
  350.2 0.9 reshape.452
  351.1 3.2 multiply_reduce_fusion.1
  354.4 16.9 %all_to_all.15 = bf16[8,16,1536]{2,1,0:T(8,128)(2,1)S(1)} all-to-all(bf16[8,16,1536]{2,1,0:T(8,128)(2,1)S(1)} %broadcast_in_dim.63), channel_id=1, replica_groups=mesh['req'=16,'blk'=8] {'blk'}, dimensions={0} | all-to-all | bytes 786432 | tf_op jit(solution)/shard_map/all_to_all | solution.py:303
  371.3 5.0 %fusion.4 = f32[128,2,1120]{0,2,1:T(8,128)S(1)} fusion(bf16[128,1536,1]{1,0,2:T(8,128)(2,1)S(1)} %bitcast.207, bf16[1536,3,1120]{0,2,1:T(8,128)(2,1)} %copy.120), kind=kOutput, calls=%fused_computation.16 | convolution fusion | flops 880803840 | bytes 8421376 | tf_op jit(solution)/shard_map/nd,dkf->nkf/dot_general | solution.py:304
  376.3 3.3 fusion.17
  379.6 13.7 %all_to_all.16 = bf16[8,16,1536]{2,1,0:T(8,128)(2,1)S(1)} all-to-all(bf16[8,16,1536]{2,1,0:T(8,128)(2,1)S(1)} %bitcast.208), channel_id=1, replica_groups=mesh['req'=16,'blk'=8] {'blk'}, dimensions={0} | all-to-all | bytes 786432 | tf_op jit(solution)/shard_map/all_to_all | solution.py:314
  393.4 0.6 fusion.37
  394.0 2.2 fusion.26
  (105 shorter events, 3.1 us)
Async XLA Ops:
  7.2 16.3 %copy-start = (bf16[1,1,16,1536]{3,2,1,0:T(8,128)(2,1)S(1)}, bf16[1,1,16,1536]{3,2,1,0:T(8,128)(2,1)}, u32[]{:S(2)}) copy-start(bf16[1,1,16,1536]{3,2,1,0:T(8,128)(2,1)} %param.14) | copy-start | bytes 147460
  7.2 86.2 %all-gather.3.cloned.1.call-start = ((), (), s32[]{:S(2)}) async-start(), calls=%async_computation.4 | async-start | bytes 11280384 | tf_op jit(solution)/shard_map/all_gather | solution.py:191
  10.2 218.4 %all-gather.5.cloned.1.call-start = ((), (), s32[]{:S(2)}) async-start(), calls=%async_computation.5 | async-start | bytes 7077888 | tf_op jit(solution)/shard_map/all_gather | solution.py:288
  13.0 6.3 %copy-start.10 = (s32[1,1,17]{2,1,0:T(1,128)S(1)}, s32[1,1,17]{2,1,0:T(1,128)}, u32[]{:S(2)}) copy-start(s32[1,1,17]{2,1,0:T(1,128)} %param.17) | copy-start | bytes 208
  13.0 6.9 %copy-start.7 = (s32[1,1,16]{2,1,0:T(1,128)S(1)}, s32[1,1,16]{2,1,0:T(1,128)}, u32[]{:S(2)}) copy-start(s32[1,1,16]{2,1,0:T(1,128)} %param.18) | copy-start | bytes 196
  13.0 9.1 %copy-start.6 = (bf16[1536]{0:T(1024)(128)(2,1)S(1)}, bf16[1536]{0:T(1024)(128)(2,1)}, u32[]{:S(2)}) copy-start(bf16[1536]{0:T(1024)(128)(2,1)} %param.23) | copy-start | bytes 9220
  13.0 9.1 %copy-start.5 = (s32[1,1,17,24]{3,1,2,0:T(1,128)S(1)}, s32[1,1,17,24]{3,1,2,0:T(1,128)}, u32[]{:S(2)}) copy-start(s32[1,1,17,24]{3,1,2,0:T(1,128)} %param.16) | copy-start | bytes 4900
  72.3 1.6 copy-start.3
  72.3 4.2 %slice-start.3 = ((s8[4718592]{0:T(1024)(128)(4,1)}), s8[4194304]{0:T(1024)(128)(4,1)S(1)}, s32[]{:S(2)}) async-start(s8[4718592]{0:T(1024)(128)(4,1)} %bitcast.189), calls=%async_computation.10 | async-start | bytes 8388608
  73.9 4.1 %slice-start = ((s8[12582912]{0:T(1024)(128)(4,1)}), s8[4194304]{0:T(1024)(128)(4,1)S(1)}, s32[]{:S(2)}) async-start(s8[12582912]{0:T(1024)(128)(4,1)} %bitcast.186), calls=%async_computation.7 | async-start | bytes 8388608
  73.9 2.7 slice-start.4
  73.9 2.7 copy-start.2
  73.9 4.1 %slice-start.1 = ((s8[12582912]{0:T(1024)(128)(4,1)}), s8[4194304]{0:T(1024)(128)(4,1)S(1)}, s32[]{:S(2)}) async-start(s8[12582912]{0:T(1024)(128)(4,1)} %bitcast.186), calls=%async_computation.8 | async-start | bytes 8388608
  74.0 5.1 %slice-start.2 = ((s8[12582912]{0:T(1024)(128)(4,1)}), s8[4194304]{0:T(1024)(128)(4,1)S(1)}, s32[]{:S(2)}) async-start(s8[12582912]{0:T(1024)(128)(4,1)} %bitcast.186), calls=%async_computation.9 | async-start | bytes 8388608
  76.5 2.6 copy-start.4
  94.7 199.9 %all-to-all-start = ((bf16[16,2,392,512]{3,2,1,0:T(8,128)(2,1)}), bf16[16,2,392,512]{3,2,1,0:T(8,128)(2,1)}, u32[]{:S(2)}, u32[]{:S(2)}) async-start(bf16[16,2,392,512]{3,2,1,0:T(8,128)(2,1)} %maximum_maximum_fusion), calls=%async_computation.1 | async-start | bytes 25690112 | tf_op jit(solution)/shard_map/all_to_all | solution.py:252
  101.1 293.0 %reduce-scatter.2.cloned.1.call-start = ((), (), s32[]{:S(2)}) async-start(), calls=%async_computation.6 | async-start | bytes 7077888 | tf_op jit(solution)/shard_map/reduce_scatter | solution.py:322
  264.1 0.7 copy-start.9
  264.1 0.8 copy-start.8
  371.3 24.9 %copy-start.1 = (bf16[1,1,16,1536]{3,2,1,0:T(8,128)(2,1)S(1)}, bf16[1,1,16,1536]{3,2,1,0:T(8,128)(2,1)}, u32[]{:S(2)}) copy-start(bf16[1,1,16,1536]{3,2,1,0:T(8,128)(2,1)} %param.14) | copy-start | bytes 147460
Sparse Core Ops, SparseCore 0:
  10.3 65.1 all-gather.2
  94.8 133.7 all-gather.4
  264.3 110.2 reduce-scatter.1

commit v4 on v1

--- a/solution.py
+++ b/solution.py
@@ -86,31 +86,34 @@
     return result.reshape(batch_count, total_rows, QUERY_HEADS * HEAD_SIZE).astype(jnp.bfloat16)
 
 
-def decode_kernel(order_ref, length_ref, cache_ref, kv_ref, q_ref, new_ref, att_ref):
-    limit = length_ref[pl.program_id(0)]
-    rows = cache_ref[...]
-    positions = lax.broadcasted_iota(jnp.int32, rows.shape, 0)
-    extended = jnp.where(
-        positions < limit,
-        rows,
-        jnp.where(positions == limit, kv_ref[...], jnp.zeros_like(rows)),
-    )
-    new_ref[...] = extended
+def decode_kernel(order_ref, length_ref, first_ref, second_ref, kv_ref, q_ref, new_ref, att_ref):
     group_width = QUERY_HEADS // KEY_VALUE_HEADS
     key_head_width = KEY_VALUE_HEADS * HEAD_SIZE
-    key_ids = lax.broadcasted_iota(jnp.int32, (group_width, rows.shape[0]), 1)
-    for head in range(KEY_VALUE_HEADS):
-        keys = extended[:, head * HEAD_SIZE : (head + 1) * HEAD_SIZE]
-        values = extended[:, key_head_width + head * HEAD_SIZE : key_head_width + (head + 1) * HEAD_SIZE]
-        scores = lax.dot_general(
-            q_ref[head], keys, (((1,), (1,)), ((), ())), preferred_element_type=jnp.float32
-        ) / math.sqrt(HEAD_SIZE)
-        scores = jnp.where(key_ids <= limit, scores, -jnp.inf)
-        weights = jnp.exp(scores - jnp.max(scores, axis=1, keepdims=True))
-        weights = (weights / jnp.sum(weights, axis=1, keepdims=True)).astype(jnp.bfloat16)
-        att_ref[head] = jnp.dot(weights, values, preferred_element_type=jnp.float32).astype(
-            jnp.bfloat16
+    for half, cache_ref in enumerate((first_ref, second_ref)):
+        limit = length_ref[2 * pl.program_id(0) + half]
+        rows = cache_ref[...]
+        positions = lax.broadcasted_iota(jnp.int32, rows.shape, 0)
+        extended = jnp.where(
+            positions < limit,
+            rows,
+            jnp.where(positions == limit, kv_ref[half], jnp.zeros_like(rows)),
         )
+        new_ref[half] = extended
+        key_ids = lax.broadcasted_iota(jnp.int32, (group_width, rows.shape[0]), 1)
+        for head in range(KEY_VALUE_HEADS):
+            keys = extended[:, head * HEAD_SIZE : (head + 1) * HEAD_SIZE]
+            values = extended[
+                :, key_head_width + head * HEAD_SIZE : key_head_width + (head + 1) * HEAD_SIZE
+            ]
+            scores = lax.dot_general(
+                q_ref[half, head], keys, (((1,), (1,)), ((), ())), preferred_element_type=jnp.float32
+            ) / math.sqrt(HEAD_SIZE)
+            scores = jnp.where(key_ids <= limit, scores, -jnp.inf)
+            weights = jnp.exp(scores - jnp.max(scores, axis=1, keepdims=True))
+            weights = (weights / jnp.sum(weights, axis=1, keepdims=True)).astype(jnp.bfloat16)
+            att_ref[half, head] = jnp.dot(
+                weights, values, preferred_element_type=jnp.float32
+            ).astype(jnp.bfloat16)
 
 
 def decode_attend(arrival_order, got_length, recv_cache, decode_kv, decode_q):
@@ -118,23 +121,23 @@
     cache_length, width_per_row = recv_cache.shape[1:]
     group_width = QUERY_HEADS // KEY_VALUE_HEADS
     order = jnp.clip(arrival_order, 0, recv_cache.shape[0] - 1)
+    head_block = (2, KEY_VALUE_HEADS, group_width, HEAD_SIZE)
     new_cache, attended = pl.pallas_call(
         decode_kernel,
         grid_spec=pltpu.PrefetchScalarGridSpec(
             num_scalar_prefetch=2,
-            grid=(count,),
+            grid=(count // 2,),
             in_specs=[
-                pl.BlockSpec((None, cache_length, width_per_row), lambda p, o, n: (o[p], 0, 0)),
-                pl.BlockSpec((None, 1, width_per_row), lambda p, o, n: (p, 0, 0)),
+                pl.BlockSpec((None, cache_length, width_per_row), lambda p, o, n: (o[2 * p], 0, 0)),
                 pl.BlockSpec(
-                    (None, KEY_VALUE_HEADS, group_width, HEAD_SIZE), lambda p, o, n: (p, 0, 0, 0)
+                    (None, cache_length, width_per_row), lambda p, o, n: (o[2 * p + 1], 0, 0)
                 ),
+                pl.BlockSpec((2, 1, width_per_row), lambda p, o, n: (p, 0, 0)),
+                pl.BlockSpec(head_block, lambda p, o, n: (p, 0, 0, 0)),
             ],
             out_specs=[
-                pl.BlockSpec((None, cache_length, width_per_row), lambda p, o, n: (p, 0, 0)),
-                pl.BlockSpec(
-                    (None, KEY_VALUE_HEADS, group_width, HEAD_SIZE), lambda p, o, n: (p, 0, 0, 0)
-                ),
+                pl.BlockSpec((2, cache_length, width_per_row), lambda p, o, n: (p, 0, 0)),
+                pl.BlockSpec(head_block, lambda p, o, n: (p, 0, 0, 0)),
             ],
         ),
         out_shape=[
@@ -144,6 +147,7 @@
     )(
         order,
         got_length,
+        recv_cache,
         recv_cache,
         decode_kv.reshape(count, 1, width_per_row),
         decode_q.reshape(count, KEY_VALUE_HEADS, group_width, HEAD_SIZE),

time: 388 us -> 386 us (level)
  no operation moved by 1% of the time
where the time goes in v4:
time: 386 us; the launch traced here: 385 us
  waiting for transfers between devices  167 us (43%)
  matrix products  61 us (16%)
  local copies, waits for them, and re-layouts  57 us (15%)
  blocking collectives  34.3 us (9%)
  other arithmetic  22.2 us (6%)
  starting transfers between devices  14.4 us (4%)
  between operations  14.4 us (4%)
  Pallas kernels  14.1 us (4%)
    all_gather x1, waiting for transfers between devices, feed_forward_partial(): lax.all_gather(mlp_in, 'blk', axis=0, tiled=True)  90.2 us
    all_to_all x1, waiting for transfers between devices, shards(): lax.all_to_all(send_cache, 'req', split_axis=0, concat_axis=0, tiled=True)  67.2 us
    gather x1, local copies, waits for them, and re-layouts, shards(): pool_rows[send_pages].reshape(n_req, CAP, cache_length, width_per_row)  22.5 us
    all_to_all x1, blocking collectives, small_feed_forward(): lax.all_to_all(spread, 'blk', split_axis=0, concat_axis=0, tiled=True)  22.4 us
    dot_general x1, matrix products, feed_forward_partial(): jnp.einsum('nd,dkf->nkf', lax.all_gather(mlp_in, 'blk', axis=0, tiled=Tru...  20.5 us
    dot_general x1, matrix products, feed_forward_partial(): jnp.einsum('nf,df->nd', hidden, all_weights[:, 2, :], preferred_element_t...  15 us
    optimization_barrier x1, local copies, waits for them, and re-layouts, shards(): lax.optimization_barrier((all_weights, prefill_res, send_cache))  14.3 us
    pallas_call x1, Pallas kernels, decode_attend(): pl.pallas_call(decode_kernel, grid_spec=pltpu.PrefetchScalarGridSpec(num_...  14.1 us
  transfers between devices with their start and end apart: 6, of which 4 were waited for; matrix products, arithmetic and copies ran while one was open for 34% of the time, Pallas kernels for 4%

profile of v4, /device:TPU:0, one launch (start us, length us, event | category | flops | bytes accessed | tf_op | source)
XLA Modules:
  0.0 384.8 jit_solution(8387911892191754741)
XLA Ops:
  7.2 1.1 copy.67
  8.3 1.9 pad_maximum_fusion
  10.2 0.7 convert_element_type.122
  10.9 0.7 convert_element_type.124
  11.6 1.4 fusion.20
  13.0 4.9 %convolution_add_fusion.1 = f32[256,2048]{1,0:T(8,128)S(1)} fusion(bf16[1536,2048]{1,0:T(8,128)(2,1)} %param.20, f32[2048]{0:T(1024)S(1)} %convert_element_type.124, bf16[1,1,256,1536]{3,2,1,0:T(8,128)(2,1)} %param.13, f32[1536]{0:T(1024)S(1)} %convert_element_type.122, f32[256]{0:T(256)S(1)} %add_rsqrt_fusion.1), kind=kOutput, calls=%fused_computation.29 | convolution fusion | flops 1612709888 | bytes 9190400 | tf_op jit(solution)/shard_map/dot_general | solution.py:38
  18.0 1.3 copy-done.2
  19.2 0.6 slice.82
  19.8 0.7 add_convert_fusion.3
  20.5 0.3 multiply_cosine_fusion
  20.9 0.6 copy-done.4
  21.9 3.6 gather_fusion
  25.4 0.3 slice_negate_fusion.1
  25.8 0.4 maximum_multiply_fusion.1
  26.2 1.0 fusion.34
  27.3 0.8 fusion.58
  28.3 0.5 copy.73
  28.9 1.0 maximum_multiply_fusion
  29.9 0.5 copy.74
  30.4 1.0 mul.270
  31.4 1.6 copy.72
  33.1 2.3 add_convert_fusion.1
  35.3 0.3 copy.75
  35.6 1.2 copy.70
  36.8 0.9 convert_reduce_fusion.2
  37.7 0.7 iota_add_fusion
  38.4 0.7 multiply_add_fusion
  39.2 0.6 gather_fusion.1
  39.9 22.5 %gather_fusion.2 = bf16[768,16,512]{2,1,0:T(8,128)(2,1)} fusion(bf16[408,16,512]{2,1,0:T(8,128)(2,1)} %bitcast.171, s32[1024]{0:T(1024)S(1)} %pad_clamp_fusion.2), kind=kCustom, calls=%fused_computation.2 | custom fusion | bytes 25168896 | tf_op jit(solution)/shard_map/gather | solution.py:210
  62.4 0.7 iota_compare_fusion.4
  63.3 1.3 fusion.7
  64.6 1.6 fusion.1
  66.3 2.5 fusion.23
  68.9 1.4 convolution_add_fusion
  70.3 5.2 %all-gather.3.cloned.1.call-done = bf16[1536,3,1120]{2,0,1:T(8,128)(2,1)} async-done(((bf16[96,3,1120]{2,0,1:T(8,128)(2,1)}), bf16[1536,3,1120]{2,0,1:T(8,128)(2,1)}) %all-gather.3.cloned.1.call-update) | async-done | bytes 10321936 | tf_op jit(solution)/shard_map/all_gather | solution.py:195
  75.7 1.1 multiply_convert_fusion
  76.8 0.7 gather_fusion.4
  77.6 0.7 broadcast_in_dim.63
  78.3 5.1 %all-to-all-start.2 = ((s32[16,2,128]{2,1,0:T(2,128)}), s32[16,2,128]{2,1,0:T(2,128)S(1)}, u32[]{:S(2)}, u32[]{:S(2)}) async-start(s32[16,2,128]{2,1,0:T(2,128)} %broadcast_in_dim.63), calls=%async_computation.3 | async-start | bytes 32768 | tf_op jit(solution)/shard_map/all_to_all | solution.py:214
  83.4 0.6 gather_fusion.3
  84.0 0.7 reshape.376
  84.7 4.7 %all-to-all-done.2 = s32[16,2,128]{2,1,0:T(2,128)S(1)} async-done(((s32[16,2,128]{2,1,0:T(2,128)}), s32[16,2,128]{2,1,0:T(2,128)S(1)}, u32[]{:S(2)}, u32[]{:S(2)}) %all-to-all-start.2) | async-done | bytes 16416 | tf_op jit(solution)/shard_map/all_to_all | solution.py:214
  89.5 3.5 all-to-all-start.1
  93.0 14.3 %copy.79 = bf16[1536,3,1120]{0,2,1:T(8,128)(2,1)} copy(bf16[1536,3,1120]{2,0,1:T(8,128)(2,1)} %all-gather.3.cloned.1.call-done) | data formatting | bytes 20643840 | tf_op jit(solution)/shard_map/optimization_barrier | solution.py:242
  107.3 5.7 %all-to-all-start = ((bf16[16,2,384,512]{3,2,1,0:T(8,128)(2,1)}), bf16[16,2,384,512]{3,2,1,0:T(8,128)(2,1)}, u32[]{:S(2)}, u32[]{:S(2)}) async-start(bf16[16,2,384,512]{3,2,1,0:T(8,128)(2,1)} %bitcast.167), calls=%async_computation.1 | async-start | bytes 25165824 | tf_op jit(solution)/shard_map/all_to_all | solution.py:245
  113.0 90.2 %all-gather.5.cloned.1.call-done = bf16[2048,1536]{1,0:T(8,128)(2,1)} async-done(((bf16[256,1536]{1,0:T(8,128)(2,1)}), bf16[2048,1536]{1,0:T(8,128)(2,1)}) %all-gather.5.cloned.1.call-update) | async-done | bytes 6291472 | tf_op jit(solution)/shard_map/all_gather | solution.py:279
  203.3 20.5 %fusion.2 = f32[2048,2,1120]{0,2,1:T(8,128)} fusion(bf16[2048,1536]{1,0:T(8,128)(2,1)} %all-gather.5.cloned.1.call-done, bf16[1536,3,1120]{0,2,1:T(8,128)(2,1)} %copy.79), kind=kOutput, calls=%fused_computation.14 | convolution fusion | flops 14092861440 | bytes 31522816 | tf_op jit(solution)/shard_map/nd,dkf->nkf/dot_general | solution.py:277
  223.7 15.0 %convolution_convert_fusion = bf16[2048,1536]{1,0:T(8,128)(2,1)} fusion(f32[2048,2,1120]{0,2,1:T(8,128)} %fusion.2, bf16[1536,3,1120]{2,0,1:T(8,128)(2,1)} %all-gather.3.cloned.1.call-done), kind=kOutput, calls=%fused_computation.12 | convolution fusion | flops 7063339008 | bytes 28180480 | tf_op jit(solution)/shard_map/nf,df->nd/dot_general | solution.py:284
  239.1 0.5 broadcast_clamp_fusion.order_ref
  239.6 67.2 %all-to-all-done = bf16[16,2,384,512]{3,2,1,0:T(8,128)(2,1)} async-done(((bf16[16,2,384,512]{3,2,1,0:T(8,128)(2,1)}), bf16[16,2,384,512]{3,2,1,0:T(8,128)(2,1)}, u32[]{:S(2)}, u32[]{:S(2)}) %all-to-all-start) | async-done | bytes 12582944 | tf_op jit(solution)/shard_map/all_to_all | solution.py:245
  306.8 0.6 gather_fusion.5
  307.5 3.8 convolution_add_fusion.3
  311.3 0.7 gather_fusion.6
  312.6 0.7 reshape.382.q_ref
  313.6 0.7 pad_maximum_fusion.3.kv_ref
  314.2 14.1 %shard_map.148 = (bf16[16,384,512]{2,1,0:T(8,128)(2,1)}, bf16[16,2,6,128]{3,2,1,0:T(8,128)(2,1)}) custom-call(s32[16]{0:T(128)} %broadcast_clamp_fusion.order_ref, s32[16]{0:T(128)} %copy-done.8, bf16[32,384,512]{2,1,0:T(8,128)(2,1)} %bitcast.41.first_ref.second_ref, bf16[32,384,512]{2,1,0:T(8,128)(2,1)} %bitcast.41.first_ref.second_ref, ...), custom_call_target="tpu_custom_call" | custom-call | tf_op jit(solution)/shard_map/pallas_call | solution.py:125
  328.3 0.9 reshape.383
  329.2 3.2 multiply_reduce_fusion.1
  332.5 22.4 %all_to_all.25 = bf16[8,16,1536]{2,1,0:T(8,128)(2,1)S(1)} all-to-all(bf16[8,16,1536]{2,1,0:T(8,128)(2,1)S(1)} %broadcast_in_dim.66), channel_id=1, replica_groups=mesh['req'=16,'blk'=8] {'blk'}, dimensions={0} | all-to-all | bytes 786432 | tf_op jit(solution)/shard_map/all_to_all | solution.py:294
  354.9 5.1 %fusion.4 = f32[128,2,1120]{0,2,1:T(8,128)S(1)} fusion(bf16[128,1536,1]{1,0,2:T(8,128)(2,1)S(1)} %bitcast.185, bf16[1536,3,1120]{0,2,1:T(8,128)(2,1)} %copy.79), kind=kOutput, calls=%fused_computation.16 | convolution fusion | flops 880803840 | bytes 8421376 | tf_op jit(solution)/shard_map/nd,dkf->nkf/dot_general | solution.py:295
  360.0 3.4 fusion.17
  363.4 12.0 %all_to_all.26 = bf16[8,16,1536]{2,1,0:T(8,128)(2,1)S(1)} all-to-all(bf16[8,16,1536]{2,1,0:T(8,128)(2,1)S(1)} %bitcast.186), channel_id=1, replica_groups=mesh['req'=16,'blk'=8] {'blk'}, dimensions={0} | all-to-all | bytes 786432 | tf_op jit(solution)/shard_map/all_to_all | solution.py:305
  375.4 0.6 fusion.39
  376.1 2.2 fusion.26
  (94 shorter events, 3.2 us)
Async XLA Ops:
  7.2 76.2 %copy-start = (bf16[1,1,16,1536]{3,2,1,0:T(8,128)(2,1)S(1)}, bf16[1,1,16,1536]{3,2,1,0:T(8,128)(2,1)}, u32[]{:S(2)}) copy-start(bf16[1,1,16,1536]{3,2,1,0:T(8,128)(2,1)} %param.14) | copy-start | bytes 147460
  7.2 68.3 %all-gather.3.cloned.1.call-start = ((), (), s32[]{:S(2)}) async-start(), calls=%async_computation.6 | async-start | bytes 11280384 | tf_op jit(solution)/shard_map/all_gather | solution.py:195
  10.2 193.1 %all-gather.5.cloned.1.call-start = ((), (), s32[]{:S(2)}) async-start(), calls=%async_computation.7 | async-start | bytes 7077888 | tf_op jit(solution)/shard_map/all_gather | solution.py:279
  13.0 6.3 %copy-start.9 = (s32[1,1,17]{2,1,0:T(1,128)S(1)}, s32[1,1,17]{2,1,0:T(1,128)}, u32[]{:S(2)}) copy-start(s32[1,1,17]{2,1,0:T(1,128)} %param.17) | copy-start | bytes 208
  13.0 8.8 %copy-start.6 = (s32[1,1,17,24]{3,1,2,0:T(1,128)S(1)}, s32[1,1,17,24]{3,1,2,0:T(1,128)}, u32[]{:S(2)}) copy-start(s32[1,1,17,24]{3,1,2,0:T(1,128)} %param.16) | copy-start | bytes 4900
  17.9 1.3 copy-start.2
  19.2 9.0 %slice-start.2 = ((f32[256,2048]{1,0:T(8,128)}), f32[256,1536]{1,0:T(8,128)S(1)}, s32[]{:S(2)}) async-start(f32[256,2048]{1,0:T(8,128)} %copy-done.2), calls=%async_computation.11 | async-start | bytes 3145728 | tf_op jit(solution)/shard_map/slice | solution.py:44
  20.8 0.7 copy-start.4
  20.8 1.0 copy-start.5
  39.9 22.6 %copy-start.7 = (bf16[1536]{0:T(1024)(128)(2,1)S(1)}, bf16[1536]{0:T(1024)(128)(2,1)}, u32[]{:S(2)}) copy-start(bf16[1536]{0:T(1024)(128)(2,1)} %param.23) | copy-start | bytes 9220
  64.6 4.2 %slice-start = ((s8[4718592]{0:T(1024)(128)(4,1)}), s8[524288]{0:T(1024)(128)(4,1)S(1)}, s32[]{:S(2)}) async-start(s8[4718592]{0:T(1024)(128)(4,1)} %bitcast.168), calls=%async_computation.9 | async-start | bytes 1048576
  66.3 2.6 slice-start.1
  66.3 2.6 copy-start.3
  68.9 7.9 %copy-start.10 = (s32[1,1,17]{2,1,0:T(1,128)S(1)}, s32[1,1,17]{2,1,0:T(1,128)}, u32[]{:S(2)}) copy-start(s32[1,1,17]{2,1,0:T(1,128)} %param.17) | copy-start | bytes 208
  78.3 11.2 %all-to-all-start.2 = ((s32[16,2,128]{2,1,0:T(2,128)}), s32[16,2,128]{2,1,0:T(2,128)S(1)}, u32[]{:S(2)}, u32[]{:S(2)}) async-start(s32[16,2,128]{2,1,0:T(2,128)} %broadcast_in_dim.63), calls=%async_computation.3 | async-start | bytes 32768 | tf_op jit(solution)/shard_map/all_to_all | solution.py:214
  89.5 17.8 %all-to-all-start.1 = ((bf16[16,2,1536]{2,1,0:T(2,128)(2,1)}), bf16[16,2,1536]{2,1,0:T(2,128)(2,1)S(1)}, u32[]{:S(2)}, u32[]{:S(2)}) async-start(bf16[16,2,1536]{2,1,0:T(2,128)(2,1)} %reshape.376), calls=%async_computation.2 | async-start | bytes 196608 | tf_op jit(solution)/shard_map/all_to_all | solution.py:213
  107.3 199.5 %all-to-all-start = ((bf16[16,2,384,512]{3,2,1,0:T(8,128)(2,1)}), bf16[16,2,384,512]{3,2,1,0:T(8,128)(2,1)}, u32[]{:S(2)}, u32[]{:S(2)}) async-start(bf16[16,2,384,512]{3,2,1,0:T(8,128)(2,1)} %bitcast.167), calls=%async_computation.1 | async-start | bytes 25165824 | tf_op jit(solution)/shard_map/all_to_all | solution.py:245
  113.0 263.1 %reduce-scatter.2.cloned.1.call-start = ((), (), s32[]{:S(2)}) async-start(), calls=%async_computation.8 | async-start | bytes 7077888 | tf_op jit(solution)/shard_map/reduce_scatter | solution.py:313
  312.0 2.2 copy-start.8
  354.9 23.4 %copy-start.1 = (bf16[1,1,16,1536]{3,2,1,0:T(8,128)(2,1)S(1)}, bf16[1,1,16,1536]{3,2,1,0:T(8,128)(2,1)}, u32[]{:S(2)}) copy-start(bf16[1,1,16,1536]{3,2,1,0:T(8,128)(2,1)} %param.14) | copy-start | bytes 147460
Sparse Core Ops, SparseCore 0:
  10.3 65.1 all-gather.2
  78.4 124.8 all-gather.4
  238.9 125.8 reduce-scatter.1

commit v5 on v4

--- a/solution.py
+++ b/solution.py
@@ -208,10 +208,12 @@
     picked = jnp.sum(jnp.where(matches, slot_ids[None, :], 0), axis=1)
     send_pages = table_rows[picked]
     send_cache = pool_rows[send_pages].reshape(n_req, CAP, cache_length, width_per_row)
-    send_x = decode_x[picked].reshape(n_req, CAP, -1)
-    send_len = jnp.broadcast_to(own_len[picked].reshape(n_req, CAP, 1), (n_req, CAP, 128))
+    sent_len = own_len[picked]
+    length_code = jnp.stack([sent_len // 16, sent_len % 16], axis=1).astype(jnp.bfloat16)
+    send_x = jnp.concatenate(
+        [decode_x[picked], jnp.pad(length_code, ((0, 0), (0, 126)))], axis=1
+    ).reshape(n_req, CAP, -1)
     recv_x = lax.all_to_all(send_x, "req", split_axis=0, concat_axis=0, tiled=True)
-    recv_len = lax.all_to_all(send_len, "req", split_axis=0, concat_axis=0, tiled=True)
 
     shift = jnp.mod(send_dest - own_index, n_req)
     source = jnp.mod(own_index - shift, n_req)
@@ -244,12 +246,12 @@
     )
     recv_cache = lax.all_to_all(send_cache, "req", split_axis=0, concat_axis=0, tiled=True)
     prefill_partial = feed_forward_partial(prefill_res, mlp_gain, all_weights)
-    _, recv_cache, recv_x, recv_len = lax.optimization_barrier(
-        (prefill_partial, recv_cache, recv_x, recv_len)
-    )
+    _, recv_cache, recv_x = lax.optimization_barrier((prefill_partial, recv_cache, recv_x))
     prefill_out = feed_forward_finish(prefill_res, prefill_partial)
-    got_x = recv_x.reshape(n_req * CAP, -1)[arrival_order]
-    got_length = recv_len.reshape(n_req * CAP, 128)[arrival_order, 0]
+    got_row = recv_x.reshape(n_req * CAP, -1)[arrival_order]
+    got_x = got_row[:, : decode_x.shape[1]]
+    got_code = got_row[:, decode_x.shape[1] : decode_x.shape[1] + 2].astype(jnp.int32)
+    got_length = got_code[:, 0] * 16 + got_code[:, 1]
 
     decode_q, decode_kv = project(
         rms_scale(got_x, attn_gain), inproj_weight, inproj_bias, got_length

time: 386 us -> 377 us (0.977)
  waiting for transfers between devices: 167 us -> 154 us
  local copies, waits for them, and re-layouts: 57 us -> 64.3 us
    all_to_all x1, waiting for transfers between devices: 67.2 us -> 57.6 us  [shards(): lax.all_to_all(send_cache, 'req', split_axis=0, concat_axis=0, tiled=True)]
    all_gather x1, waiting for transfers between devices: 90.2 us -> 96.7 us  [feed_forward_partial(): lax.all_gather(mlp_in, 'blk', axis=0, tiled=True)]
    all_gather x1, waiting for transfers between devices: 5.21 us -> 0.02 us  [shards(): lax.all_gather(jnp.concatenate([gate_up, local_down], axis=1), 'req', axi...]
    mul x6, local copies, waits for them, and re-layouts: 3.25 us -> 8.38 us  [apply_rotary(): return vectors * cosine + turned * sine_table]
    all_to_all x1 -> x0, starting transfers between devices: 5.08 us -> none  [shards(): lax.all_to_all(send_len, 'req', split_axis=0, concat_axis=0, tiled=True)]
    all_to_all x1 -> x0, waiting for transfers between devices: 4.74 us -> none  [shards(): lax.all_to_all(send_len, 'req', split_axis=0, concat_axis=0, tiled=True)]
    slice x4 -> x3, local copies, waits for them, and re-layouts: 0.48 us -> 4.4 us  [project(): mixed_batch[:, :query_head_width].reshape(-1, QUERY_HEADS, HEAD_SIZE)]
  transfers between devices with their start and end apart: 6 -> 5, of which waited for: 4 -> 2; matrix products, arithmetic and copies ran while one was open for 34% -> 38% of each run, Pallas kernels for 4% -> 4%
where the time goes in v5:
time: 377 us; the launch traced here: 376 us
  waiting for transfers between devices  154 us (41%)
  local copies, waits for them, and re-layouts  64.3 us (17%)
  matrix products  61.2 us (16%)
  blocking collectives  32.6 us (9%)
  other arithmetic  22.7 us (6%)
  between operations  14.3 us (4%)
  Pallas kernels  14.1 us (4%)
  starting transfers between devices  12.3 us (3%)
    all_gather x1, waiting for transfers between devices, feed_forward_partial(): lax.all_gather(mlp_in, 'blk', axis=0, tiled=True)  96.7 us
    all_to_all x1, waiting for transfers between devices, shards(): lax.all_to_all(send_cache, 'req', split_axis=0, concat_axis=0, tiled=True)  57.6 us
    gather x1, local copies, waits for them, and re-layouts, shards(): pool_rows[send_pages].reshape(n_req, CAP, cache_length, width_per_row)  22.7 us
    all_to_all x1, blocking collectives, small_feed_forward(): lax.all_to_all(spread, 'blk', split_axis=0, concat_axis=0, tiled=True)  20.6 us
    dot_general x1, matrix products, feed_forward_partial(): jnp.einsum('nd,dkf->nkf', lax.all_gather(mlp_in, 'blk', axis=0, tiled=Tru...  20.5 us
    dot_general x1, matrix products, feed_forward_partial(): jnp.einsum('nf,df->nd', hidden, all_weights[:, 2, :], preferred_element_t...  15 us
    optimization_barrier x1, local copies, waits for them, and re-layouts, shards(): lax.optimization_barrier((all_weights, prefill_res, send_cache))  14.4 us
    pallas_call x1, Pallas kernels, decode_attend(): pl.pallas_call(decode_kernel, grid_spec=pltpu.PrefetchScalarGridSpec(num_...  14.1 us
  transfers between devices with their start and end apart: 5, of which 2 were waited for; matrix products, arithmetic and copies ran while one was open for 38% of the time, Pallas kernels for 4%

profile of v5, /device:TPU:0, one launch (start us, length us, event | category | flops | bytes accessed | tf_op | source)
XLA Modules:
  0.0 375.8 jit_solution(3903394147337257585)
XLA Ops:
  7.2 1.1 copy.95
  8.3 1.9 pad_maximum_fusion
  10.2 0.7 convert_element_type.125
  10.9 0.7 convert_element_type.127
  11.6 1.4 fusion.20
  13.0 4.9 %convolution_add_fusion.1 = f32[256,2048]{1,0:T(8,128)S(1)} fusion(bf16[1536,2048]{1,0:T(8,128)(2,1)} %param.20, f32[2048]{0:T(1024)S(1)} %convert_element_type.127, bf16[1,1,256,1536]{3,2,1,0:T(8,128)(2,1)} %param.13, f32[1536]{0:T(1024)S(1)} %convert_element_type.125, f32[256]{0:T(256)S(1)} %add_rsqrt_fusion.1), kind=kOutput, calls=%fused_computation.28 | convolution fusion | flops 1612709888 | bytes 9190400 | tf_op jit(solution)/shard_map/dot_general | solution.py:38
  18.0 1.3 slice.139
  19.3 0.6 slice.94
  19.9 0.7 add_convert_fusion.3
  20.5 0.3 multiply_cosine_fusion
  20.9 0.7 copy.97
  21.7 0.8 copy.96
  22.5 3.5 gather_fusion
  26.0 0.3 slice_negate_fusion.1
  26.3 1.3 maximum_multiply_fusion.1
  27.6 1.0 mul.271
  28.7 0.8 fusion.64
  29.5 0.2 copy.99
  29.7 3.1 copy.101
  32.8 1.5 slice_negate_fusion
  34.3 1.3 maximum_multiply_fusion
  35.5 3.1 copy.102
  38.6 1.3 mul.277
  39.9 3.0 copy.100
  42.9 2.2 add_convert_fusion.1
  45.1 0.3 copy.103
  45.4 1.2 copy.98
  46.6 0.2 convert_reduce_fusion.3
  46.9 0.6 gather_fusion.1
  47.6 22.7 %gather_fusion.2 = bf16[768,16,512]{2,1,0:T(8,128)(2,1)} fusion(bf16[408,16,512]{2,1,0:T(8,128)(2,1)} %bitcast.181, s32[1024]{0:T(1024)S(1)} %pad_clamp_fusion.2), kind=kCustom, calls=%fused_computation.2 | custom fusion | bytes 25168896 | tf_op jit(solution)/shard_map/gather | solution.py:210
  70.3 0.7 iota_compare_fusion.5
  71.2 1.3 fusion.7
  72.5 1.6 fusion.1
  74.2 2.5 fusion.23
  76.7 1.4 convolution_add_fusion
  78.2 0.2 multiply_reduce_fusion
  78.4 1.1 multiply_convert_fusion
  79.5 0.7 gather_fusion.4
  80.3 0.6 gather_fusion.3
  81.0 0.7 reshape.443
  81.7 6.5 %all-to-all-start.1 = ((bf16[16,2,1664]{2,1,0:T(2,128)(2,1)}), bf16[16,2,1664]{2,1,0:T(2,128)(2,1)S(1)}, u32[]{:S(2)}, u32[]{:S(2)}) async-start(bf16[16,2,1664]{2,1,0:T(2,128)(2,1)} %reshape.443), calls=%async_computation.2 | async-start | bytes 212992 | tf_op jit(solution)/shard_map/all_to_all | solution.py:216
  88.2 14.4 %copy.107 = bf16[1536,3,1120]{0,2,1:T(8,128)(2,1)} copy(bf16[1536,3,1120]{2,0,1:T(8,128)(2,1)} %all-gather.3.cloned.1.call-done) | data formatting | bytes 20643840 | tf_op jit(solution)/shard_map/optimization_barrier | solution.py:244
  102.6 5.7 %all-to-all-start = ((bf16[16,2,384,512]{3,2,1,0:T(8,128)(2,1)}), bf16[16,2,384,512]{3,2,1,0:T(8,128)(2,1)}, u32[]{:S(2)}, u32[]{:S(2)}) async-start(bf16[16,2,384,512]{3,2,1,0:T(8,128)(2,1)} %bitcast.177), calls=%async_computation.1 | async-start | bytes 25165824 | tf_op jit(solution)/shard_map/all_to_all | solution.py:247
  108.3 96.7 %all-gather.5.cloned.1.call-done = bf16[2048,1536]{1,0:T(8,128)(2,1)} async-done(((bf16[256,1536]{1,0:T(8,128)(2,1)}), bf16[2048,1536]{1,0:T(8,128)(2,1)}) %all-gather.5.cloned.1.call-update) | async-done | bytes 6291472 | tf_op jit(solution)/shard_map/all_gather | solution.py:281
  205.0 20.5 %fusion.2 = f32[2048,2,1120]{0,2,1:T(8,128)} fusion(bf16[2048,1536]{1,0:T(8,128)(2,1)} %all-gather.5.cloned.1.call-done, bf16[1536,3,1120]{0,2,1:T(8,128)(2,1)} %copy.107), kind=kOutput, calls=%fused_computation.13 | convolution fusion | flops 14092861440 | bytes 31522816 | tf_op jit(solution)/shard_map/nd,dkf->nkf/dot_general | solution.py:279
  225.5 15.0 %convolution_convert_fusion = bf16[2048,1536]{1,0:T(8,128)(2,1)} fusion(f32[2048,2,1120]{0,2,1:T(8,128)} %fusion.2, bf16[1536,3,1120]{2,0,1:T(8,128)(2,1)} %all-gather.3.cloned.1.call-done), kind=kOutput, calls=%fused_computation.11 | convolution fusion | flops 7063339008 | bytes 28180480 | tf_op jit(solution)/shard_map/nf,df->nd/dot_general | solution.py:286
  240.5 0.2 convert_reduce_fusion.2
  240.9 0.6 broadcast_clamp_fusion.order_ref
  241.4 57.6 %all-to-all-done = bf16[16,2,384,512]{3,2,1,0:T(8,128)(2,1)} async-done(((bf16[16,2,384,512]{3,2,1,0:T(8,128)(2,1)}), bf16[16,2,384,512]{3,2,1,0:T(8,128)(2,1)}, u32[]{:S(2)}, u32[]{:S(2)}) %all-to-all-start) | async-done | bytes 12582944 | tf_op jit(solution)/shard_map/all_to_all | solution.py:247
  299.1 0.6 gather_fusion.5
  299.8 4.0 %convolution_add_fusion.3 = f32[16,2048]{1,0:T(8,128)S(1)} fusion(bf16[1536,2048]{1,0:T(8,128)(2,1)} %param.20, f32[2048]{0:T(1024)S(1)} %convert_element_type.127, f32[1536]{0:T(1024)S(1)} %convert_element_type.125, f32[16]{0:T(128)S(1)} %add_rsqrt_fusion.3, bf16[16,1664]{1,0:T(8,128)(2,1)S(1)} %gather_fusion.5), kind=kOutput, calls=%fused_computation.33 | convolution fusion | flops 100794368 | bytes 6488576 | tf_op jit(solution)/shard_map/dot_general | solution.py:38
  303.9 0.2 convert_reduce_fusion.1
  304.7 0.7 reshape.448.q_ref
  305.7 0.7 fusion.50.length_ref
  306.4 0.7 pad_maximum_fusion.3.kv_ref
  307.0 14.1 %shard_map.148 = (bf16[16,384,512]{2,1,0:T(8,128)(2,1)}, bf16[16,2,6,128]{3,2,1,0:T(8,128)(2,1)}) custom-call(s32[16]{0:T(128)} %broadcast_clamp_fusion.order_ref, s32[16]{0:T(128)} %fusion.50.length_ref, bf16[32,384,512]{2,1,0:T(8,128)(2,1)} %bitcast.40.first_ref.second_ref, bf16[32,384,512]{2,1,0:T(8,128)(2,1)} %bitcast.40.first_ref.second_ref, ...), custom_call_target="tpu_custom_call" | custom-call | tf_op jit(solution)/shard_map/pallas_call | solution.py:125
  321.1 0.9 reshape.449
  322.0 3.2 multiply_reduce_fusion.1
  325.4 20.6 %all_to_all.20 = bf16[8,16,1536]{2,1,0:T(8,128)(2,1)S(1)} all-to-all(bf16[8,16,1536]{2,1,0:T(8,128)(2,1)S(1)} %broadcast_in_dim.60), channel_id=1, replica_groups=mesh['req'=16,'blk'=8] {'blk'}, dimensions={0} | all-to-all | bytes 786432 | tf_op jit(solution)/shard_map/all_to_all | solution.py:296
  346.0 5.0 %fusion.4 = f32[128,2,1120]{0,2,1:T(8,128)S(1)} fusion(bf16[128,1536,1]{1,0,2:T(8,128)(2,1)S(1)} %bitcast.194, bf16[1536,3,1120]{0,2,1:T(8,128)(2,1)} %copy.107), kind=kOutput, calls=%fused_computation.15 | convolution fusion | flops 880803840 | bytes 8421376 | tf_op jit(solution)/shard_map/nd,dkf->nkf/dot_general | solution.py:297
  351.0 3.4 fusion.17
  354.4 12.0 %all_to_all.21 = bf16[8,16,1536]{2,1,0:T(8,128)(2,1)S(1)} all-to-all(bf16[8,16,1536]{2,1,0:T(8,128)(2,1)S(1)} %bitcast.195), channel_id=1, replica_groups=mesh['req'=16,'blk'=8] {'blk'}, dimensions={0} | all-to-all | bytes 786432 | tf_op jit(solution)/shard_map/all_to_all | solution.py:307
  366.4 0.6 fusion.41
  367.0 2.2 fusion.26
  (88 shorter events, 2.5 us)
Async XLA Ops:
  7.2 73.2 %copy-start = (bf16[1,1,16,1536]{3,2,1,0:T(8,128)(2,1)S(1)}, bf16[1,1,16,1536]{3,2,1,0:T(8,128)(2,1)}, u32[]{:S(2)}) copy-start(bf16[1,1,16,1536]{3,2,1,0:T(8,128)(2,1)} %param.14) | copy-start | bytes 147460
  7.2 71.0 %all-gather.3.cloned.1.call-start = ((), (), s32[]{:S(2)}) async-start(), calls=%async_computation.5 | async-start | bytes 11280384 | tf_op jit(solution)/shard_map/all_gather | solution.py:195
  10.2 194.8 %all-gather.5.cloned.1.call-start = ((), (), s32[]{:S(2)}) async-start(), calls=%async_computation.6 | async-start | bytes 7077888 | tf_op jit(solution)/shard_map/all_gather | solution.py:281
  13.0 6.3 %copy-start.6 = (s32[1,1,17]{2,1,0:T(1,128)S(1)}, s32[1,1,17]{2,1,0:T(1,128)}, u32[]{:S(2)}) copy-start(s32[1,1,17]{2,1,0:T(1,128)} %param.17) | copy-start | bytes 208
  13.0 9.5 %copy-start.3 = (s32[1,1,17,24]{3,1,2,0:T(1,128)S(1)}, s32[1,1,17,24]{3,1,2,0:T(1,128)}, u32[]{:S(2)}) copy-start(s32[1,1,17,24]{3,1,2,0:T(1,128)} %param.16) | copy-start | bytes 4900
  38.6 8.0 %copy-start.5 = (s32[1,1,16]{2,1,0:T(1,128)S(1)}, s32[1,1,16]{2,1,0:T(1,128)}, u32[]{:S(2)}) copy-start(s32[1,1,16]{2,1,0:T(1,128)} %param.18) | copy-start | bytes 196
  47.6 22.7 %copy-start.4 = (bf16[1536]{0:T(1024)(128)(2,1)S(1)}, bf16[1536]{0:T(1024)(128)(2,1)}, u32[]{:S(2)}) copy-start(bf16[1536]{0:T(1024)(128)(2,1)} %param.23) | copy-start | bytes 9220
  72.5 4.2 %slice-start = ((s8[4718592]{0:T(1024)(128)(4,1)}), s8[524288]{0:T(1024)(128)(4,1)S(1)}, s32[]{:S(2)}) async-start(s8[4718592]{0:T(1024)(128)(4,1)} %bitcast.178), calls=%async_computation.8 | async-start | bytes 1048576
  74.2 2.6 slice-start.1
  74.2 2.5 copy-start.2
  76.7 2.8 copy-start.7
  81.7 20.9 %all-to-all-start.1 = ((bf16[16,2,1664]{2,1,0:T(2,128)(2,1)}), bf16[16,2,1664]{2,1,0:T(2,128)(2,1)S(1)}, u32[]{:S(2)}, u32[]{:S(2)}) async-start(bf16[16,2,1664]{2,1,0:T(2,128)(2,1)} %reshape.443), calls=%async_computation.2 | async-start | bytes 212992 | tf_op jit(solution)/shard_map/all_to_all | solution.py:216
  102.6 196.5 %all-to-all-start = ((bf16[16,2,384,512]{3,2,1,0:T(8,128)(2,1)}), bf16[16,2,384,512]{3,2,1,0:T(8,128)(2,1)}, u32[]{:S(2)}, u32[]{:S(2)}) async-start(bf16[16,2,384,512]{3,2,1,0:T(8,128)(2,1)} %bitcast.177), calls=%async_computation.1 | async-start | bytes 25165824 | tf_op jit(solution)/shard_map/all_to_all | solution.py:247
  108.3 258.8 %reduce-scatter.2.cloned.1.call-start = ((), (), s32[]{:S(2)}) async-start(), calls=%async_computation.7 | async-start | bytes 7077888 | tf_op jit(solution)/shard_map/reduce_scatter | solution.py:315
  346.0 23.2 %copy-start.1 = (bf16[1,1,16,1536]{3,2,1,0:T(8,128)(2,1)S(1)}, bf16[1,1,16,1536]{3,2,1,0:T(8,128)(2,1)}, u32[]{:S(2)}) copy-start(bf16[1,1,16,1536]{3,2,1,0:T(8,128)(2,1)} %param.14) | copy-start | bytes 147460
Sparse Core Ops, SparseCore 0:
  10.3 65.2 all-gather.2
  79.6 125.3 all-gather.4
  240.7 118.0 reduce-scatter.1

commit v6 on v5

--- a/solution.py
+++ b/solution.py
@@ -208,12 +208,12 @@
     picked = jnp.sum(jnp.where(matches, slot_ids[None, :], 0), axis=1)
     send_pages = table_rows[picked]
     send_cache = pool_rows[send_pages].reshape(n_req, CAP, cache_length, width_per_row)
-    sent_len = own_len[picked]
+    sent_len = own_len
     length_code = jnp.stack([sent_len // 16, sent_len % 16], axis=1).astype(jnp.bfloat16)
-    send_x = jnp.concatenate(
-        [decode_x[picked], jnp.pad(length_code, ((0, 0), (0, 126)))], axis=1
-    ).reshape(n_req, CAP, -1)
-    recv_x = lax.all_to_all(send_x, "req", split_axis=0, concat_axis=0, tiled=True)
+    coded_rows = jnp.concatenate(
+        [decode_x, jnp.pad(length_code, ((0, 0), (0, 126)))], axis=1
+    )
+    recv_x = lax.all_gather(coded_rows, "req", axis=0, tiled=True)
 
     shift = jnp.mod(send_dest - own_index, n_req)
     source = jnp.mod(own_index - shift, n_req)
@@ -248,7 +248,8 @@
     prefill_partial = feed_forward_partial(prefill_res, mlp_gain, all_weights)
     _, recv_cache, recv_x = lax.optimization_barrier((prefill_partial, recv_cache, recv_x))
     prefill_out = feed_forward_finish(prefill_res, prefill_partial)
-    got_row = recv_x.reshape(n_req * CAP, -1)[arrival_order]
+    arrival_rows = jnp.sum(jnp.where(chosen, (source * slot_total + slot_ids)[None, :], 0), axis=1)
+    got_row = recv_x[arrival_rows]
     got_x = got_row[:, : decode_x.shape[1]]
     got_code = got_row[:, decode_x.shape[1] : decode_x.shape[1] + 2].astype(jnp.int32)
     got_length = got_code[:, 0] * 16 + got_code[:, 1]

time: 377 us -> 384 us (1.019)
  blocking collectives: 32.6 us -> 98.3 us
  waiting for transfers between devices: 154 us -> 115 us
  local copies, waits for them, and re-layouts: 64.3 us -> 54.1 us
  starting transfers between devices: 12.3 us -> 5.27 us
    all_gather x0 -> x1, blocking collectives: none -> 60.9 us  [shards(): recv_x = lax.all_gather(coded_rows, 'req', axis=0, tiled=True)]
    all_to_all x1, waiting for transfers between devices: 57.6 us -> 0.01 us  [shards(): lax.all_to_all(send_cache, 'req', split_axis=0, concat_axis=0, tiled=True)]
    all_gather x1, waiting for transfers between devices: 96.7 us -> 107 us  [feed_forward_partial(): lax.all_gather(mlp_in, 'blk', axis=0, tiled=True)]
    all_gather x1, waiting for transfers between devices: 0.02 us -> 7.07 us  [shards(): lax.all_gather(jnp.concatenate([gate_up, local_down], axis=1), 'req', axi...]
    all_to_all x1 -> x0, starting transfers between devices: 6.45 us -> none  [shards(): lax.all_to_all(send_x, 'req', split_axis=0, concat_axis=0, tiled=True)]
    mul x6, local copies, waits for them, and re-layouts: 8.38 us -> 3.24 us  [apply_rotary(): return vectors * cosine + turned * sine_table]
    slice x3 -> x4, local copies, waits for them, and re-layouts: 4.4 us -> 0.48 us  [project(): mixed_batch[:, :query_head_width].reshape(-1, QUERY_HEADS, HEAD_SIZE)]
  transfers between devices with their start and end apart: 5 -> 4, of which waited for: 2 -> 2; matrix products, arithmetic and copies ran while one was open for 38% -> 33% of each run, Pallas kernels for 4% -> 4%
where the time goes in v6:
time: 384 us; the launch traced here: 383 us
  waiting for transfers between devices  115 us (30%)
  blocking collectives  98.3 us (26%)
  matrix products  60.9 us (16%)
  local copies, waits for them, and re-layouts  54.1 us (14%)
  other arithmetic  21.3 us (6%)
  between operations  14.4 us (4%)
  Pallas kernels  14.1 us (4%)
  starting transfers between devices  5.27 us (1%)
    all_gather x1, waiting for transfers between devices, feed_forward_partial(): lax.all_gather(mlp_in, 'blk', axis=0, tiled=True)  107 us
    all_gather x1, blocking collectives, shards(): recv_x = lax.all_gather(coded_rows, 'req', axis=0, tiled=True)  60.9 us
    all_to_all x1, blocking collectives, small_feed_forward(): lax.all_to_all(spread, 'blk', split_axis=0, concat_axis=0, tiled=True)  24.3 us
    gather x1, local copies, waits for them, and re-layouts, shards(): pool_rows[send_pages].reshape(n_req, CAP, cache_length, width_per_row)  22.7 us
    dot_general x1, matrix products, feed_forward_partial(): jnp.einsum('nd,dkf->nkf', lax.all_gather(mlp_in, 'blk', axis=0, tiled=Tru...  20.5 us
    dot_general x1, matrix products, feed_forward_partial(): jnp.einsum('nf,df->nd', hidden, all_weights[:, 2, :], preferred_element_t...  15 us
    optimization_barrier x1, local copies, waits for them, and re-layouts, shards(): lax.optimization_barrier((all_weights, prefill_res, send_cache))  14.3 us
    pallas_call x1, Pallas kernels, decode_attend(): pl.pallas_call(decode_kernel, grid_spec=pltpu.PrefetchScalarGridSpec(num_...  14.1 us
  transfers between devices with their start and end apart: 4, of which 2 were waited for; matrix products, arithmetic and copies ran while one was open for 33% of the time, Pallas kernels for 4%

profile of v6, /device:TPU:0, one launch (start us, length us, event | category | flops | bytes accessed | tf_op | source)
XLA Modules:
  0.0 382.9 jit_solution(15970256088369954951)
XLA Ops:
  7.2 1.1 copy.98
  8.3 1.9 pad_maximum_fusion
  10.2 0.7 convert_element_type.125
  10.9 0.7 convert_element_type.127
  11.6 1.4 fusion.20
  13.0 4.9 %convolution_add_fusion.1 = f32[256,2048]{1,0:T(8,128)S(1)} fusion(bf16[1536,2048]{1,0:T(8,128)(2,1)} %param.20, f32[2048]{0:T(1024)S(1)} %convert_element_type.127, bf16[1,1,256,1536]{3,2,1,0:T(8,128)(2,1)} %param.13, f32[1536]{0:T(1024)S(1)} %convert_element_type.125, f32[256]{0:T(256)S(1)} %add_rsqrt_fusion.1), kind=kOutput, calls=%fused_computation.26 | convolution fusion | flops 1612709888 | bytes 9190400 | tf_op jit(solution)/shard_map/dot_general | solution.py:38
  18.0 1.3 copy-done
  19.2 0.6 slice.94
  19.8 0.7 add_convert_fusion.3
  20.5 0.3 multiply_cosine_fusion
  20.8 0.6 copy-done.2
  21.6 0.1 reshape.450
  21.8 3.6 gather_fusion
  25.4 0.3 slice_negate_fusion.1
  25.8 0.4 maximum_multiply_fusion.1
  26.2 1.0 fusion.34
  27.3 0.8 fusion.63
  28.0 0.2 copy.102
  28.2 0.5 copy.104
  28.8 1.0 maximum_multiply_fusion
  29.9 0.5 copy.105
  30.3 1.0 mul.278
  31.4 1.6 copy.103
  33.0 2.3 add_convert_fusion.1
  35.3 0.3 copy.106
  35.6 1.2 copy.101
  36.8 0.2 convert_reduce_fusion.3
  37.1 0.6 gather_fusion.1
  37.8 22.7 %gather_fusion.2 = bf16[768,16,512]{2,1,0:T(8,128)(2,1)} fusion(bf16[408,16,512]{2,1,0:T(8,128)(2,1)} %bitcast.157, s32[1024]{0:T(1024)S(1)} %pad_clamp_fusion.1), kind=kCustom, calls=%fused_computation.2 | custom fusion | bytes 25168896 | tf_op jit(solution)/shard_map/gather | solution.py:210
  60.6 0.7 iota_compare_fusion.5
  61.3 0.2 pad_add_fusion
  61.4 1.3 fusion.7
  62.8 1.6 fusion.1
  64.4 2.5 fusion.23
  67.0 1.4 convolution_add_fusion
  68.4 7.1 %all-gather.3.cloned.1.call-done = bf16[1536,3,1120]{2,0,1:T(8,128)(2,1)} async-done(((bf16[96,3,1120]{2,0,1:T(8,128)(2,1)}), bf16[1536,3,1120]{2,0,1:T(8,128)(2,1)}) %all-gather.3.cloned.1.call-update) | async-done | bytes 10321936 | tf_op jit(solution)/shard_map/all_gather | solution.py:195
  75.5 0.2 multiply_reduce_fusion
  75.7 1.1 multiply_convert_fusion
  76.8 14.3 %copy.110 = bf16[1536,3,1120]{0,2,1:T(8,128)(2,1)} copy(bf16[1536,3,1120]{2,0,1:T(8,128)(2,1)} %all-gather.3.cloned.1.call-done) | data formatting | bytes 20643840 | tf_op jit(solution)/shard_map/optimization_barrier | solution.py:244
  91.1 5.1 %all-to-all-start = ((bf16[16,2,384,512]{3,2,1,0:T(8,128)(2,1)}), bf16[16,2,384,512]{3,2,1,0:T(8,128)(2,1)}, u32[]{:S(2)}, u32[]{:S(2)}) async-start(bf16[16,2,384,512]{3,2,1,0:T(8,128)(2,1)} %bitcast.153), calls=%async_computation.1 | async-start | bytes 25165824 | tf_op jit(solution)/shard_map/all_to_all | solution.py:247
  96.3 107.5 %all-gather.5.cloned.1.call-done = bf16[2048,1536]{1,0:T(8,128)(2,1)} async-done(((bf16[256,1536]{1,0:T(8,128)(2,1)}), bf16[2048,1536]{1,0:T(8,128)(2,1)}) %all-gather.5.cloned.1.call-update) | async-done | bytes 6291472 | tf_op jit(solution)/shard_map/all_gather | solution.py:282
  203.8 20.5 %fusion.2 = f32[2048,2,1120]{0,2,1:T(8,128)} fusion(bf16[2048,1536]{1,0:T(8,128)(2,1)} %all-gather.5.cloned.1.call-done, bf16[1536,3,1120]{0,2,1:T(8,128)(2,1)} %copy.110), kind=kOutput, calls=%fused_computation.11 | convolution fusion | flops 14092861440 | bytes 31522816 | tf_op jit(solution)/shard_map/nd,dkf->nkf/dot_general | solution.py:280
  224.3 15.0 %convolution_convert_fusion = bf16[2048,1536]{1,0:T(8,128)(2,1)} fusion(f32[2048,2,1120]{0,2,1:T(8,128)} %fusion.2, bf16[1536,3,1120]{2,0,1:T(8,128)(2,1)} %all-gather.3.cloned.1.call-done), kind=kOutput, calls=%fused_computation.9 | convolution fusion | flops 7063339008 | bytes 28180480 | tf_op jit(solution)/shard_map/nf,df->nd/dot_general | solution.py:287
  239.7 0.2 convert_reduce_fusion.2
  239.9 0.1 select_reduce_fusion.1
  240.3 0.6 broadcast_clamp_fusion.order_ref
  240.9 60.9 %all_gather.11 = bf16[256,1664]{1,0:T(8,128)(2,1)S(1)} all-gather(bf16[16,1664]{1,0:T(8,128)(2,1)S(1)} %fusion.40), channel_id=1, replica_groups=mesh['req'=16,'blk'=8] {'req'}, dimensions={0}, use_global_device_ids=true | all-gather | bytes 905216 | tf_op jit(solution)/shard_map/all_gather | solution.py:216
  301.8 0.6 gather_fusion.3
  302.4 0.1 fusion.36
  302.5 3.8 convolution_add_fusion.3
  306.3 0.2 convert_reduce_fusion.1
  306.5 0.1 multiply_cosine_fusion.1
  307.1 0.7 reshape.460.q_ref
  308.1 0.7 fusion.53.length_ref
  308.8 0.7 pad_maximum_fusion.3.kv_ref
  309.4 14.1 %shard_map.148 = (bf16[16,384,512]{2,1,0:T(8,128)(2,1)}, bf16[16,2,6,128]{3,2,1,0:T(8,128)(2,1)}) custom-call(s32[16]{0:T(128)} %broadcast_clamp_fusion.order_ref, s32[16]{0:T(128)} %fusion.53.length_ref, bf16[32,384,512]{2,1,0:T(8,128)(2,1)} %bitcast.37.first_ref.second_ref, bf16[32,384,512]{2,1,0:T(8,128)(2,1)} %bitcast.37.first_ref.second_ref, ...), custom_call_target="tpu_custom_call" | custom-call | tf_op jit(solution)/shard_map/pallas_call | solution.py:125
  323.5 0.9 reshape.461
  324.4 3.2 multiply_reduce_fusion.1
  327.7 24.3 %all_to_all.15 = bf16[8,16,1536]{2,1,0:T(8,128)(2,1)S(1)} all-to-all(bf16[8,16,1536]{2,1,0:T(8,128)(2,1)S(1)} %broadcast_in_dim.64), channel_id=1, replica_groups=mesh['req'=16,'blk'=8] {'blk'}, dimensions={0} | all-to-all | bytes 786432 | tf_op jit(solution)/shard_map/all_to_all | solution.py:297
  352.0 5.0 %fusion.4 = f32[128,2,1120]{0,2,1:T(8,128)S(1)} fusion(bf16[128,1536,1]{1,0,2:T(8,128)(2,1)S(1)} %bitcast.170, bf16[1536,3,1120]{0,2,1:T(8,128)(2,1)} %copy.110), kind=kOutput, calls=%fused_computation.13 | convolution fusion | flops 880803840 | bytes 8421376 | tf_op jit(solution)/shard_map/nd,dkf->nkf/dot_general | solution.py:298
  357.0 3.4 fusion.17
  360.4 13.1 %all_to_all.16 = bf16[8,16,1536]{2,1,0:T(8,128)(2,1)S(1)} all-to-all(bf16[8,16,1536]{2,1,0:T(8,128)(2,1)S(1)} %bitcast.171), channel_id=1, replica_groups=mesh['req'=16,'blk'=8] {'blk'}, dimensions={0} | all-to-all | bytes 786432 | tf_op jit(solution)/shard_map/all_to_all | solution.py:308
  373.5 0.6 fusion.41
  374.2 2.2 fusion.26
  (92 shorter events, 2.5 us)
Async XLA Ops:
  7.2 68.3 %all-gather.3.cloned.1.call-start = ((), (), s32[]{:S(2)}) async-start(), calls=%async_computation.4 | async-start | bytes 11280384 | tf_op jit(solution)/shard_map/all_gather | solution.py:195
  10.2 193.6 %all-gather.5.cloned.1.call-start = ((), (), s32[]{:S(2)}) async-start(), calls=%async_computation.5 | async-start | bytes 7077888 | tf_op jit(solution)/shard_map/all_gather | solution.py:282
  13.0 6.3 %copy-start.8 = (s32[1,1,17]{2,1,0:T(1,128)S(1)}, s32[1,1,17]{2,1,0:T(1,128)}, u32[]{:S(2)}) copy-start(s32[1,1,17]{2,1,0:T(1,128)} %param.17) | copy-start | bytes 208
  13.0 8.8 %copy-start.5 = (s32[1,1,17,24]{3,1,2,0:T(1,128)S(1)}, s32[1,1,17,24]{3,1,2,0:T(1,128)}, u32[]{:S(2)}) copy-start(s32[1,1,17,24]{3,1,2,0:T(1,128)} %param.16) | copy-start | bytes 4900
  17.9 1.3 copy-start
  19.2 9.0 %slice-start.2 = ((f32[256,2048]{1,0:T(8,128)}), f32[256,1536]{1,0:T(8,128)S(1)}, s32[]{:S(2)}) async-start(f32[256,2048]{1,0:T(8,128)} %copy-done), calls=%async_computation.9 | async-start | bytes 3145728 | tf_op jit(solution)/shard_map/slice | solution.py:44
  20.8 0.6 copy-start.2
  20.8 1.0 copy-start.3
  30.3 6.4 %copy-start.7 = (s32[1,1,16]{2,1,0:T(1,128)S(1)}, s32[1,1,16]{2,1,0:T(1,128)}, u32[]{:S(2)}) copy-start(s32[1,1,16]{2,1,0:T(1,128)} %param.18) | copy-start | bytes 196
  37.8 22.8 %copy-start.6 = (bf16[1536]{0:T(1024)(128)(2,1)S(1)}, bf16[1536]{0:T(1024)(128)(2,1)}, u32[]{:S(2)}) copy-start(bf16[1536]{0:T(1024)(128)(2,1)} %param.23) | copy-start | bytes 9220
  62.8 4.2 %slice-start = ((s8[4718592]{0:T(1024)(128)(4,1)}), s8[524288]{0:T(1024)(128)(4,1)S(1)}, s32[]{:S(2)}) async-start(s8[4718592]{0:T(1024)(128)(4,1)} %bitcast.154), calls=%async_computation.7 | async-start | bytes 1048576
  64.4 2.6 slice-start.1
  64.4 2.6 copy-start.1
  91.1 210.7 %all-to-all-start = ((bf16[16,2,384,512]{3,2,1,0:T(8,128)(2,1)}), bf16[16,2,384,512]{3,2,1,0:T(8,128)(2,1)}, u32[]{:S(2)}, u32[]{:S(2)}) async-start(bf16[16,2,384,512]{3,2,1,0:T(8,128)(2,1)} %bitcast.153), calls=%async_computation.1 | async-start | bytes 25165824 | tf_op jit(solution)/shard_map/all_to_all | solution.py:247
  96.3 277.9 %reduce-scatter.2.cloned.1.call-start = ((), (), s32[]{:S(2)}) async-start(), calls=%async_computation.6 | async-start | bytes 7077888 | tf_op jit(solution)/shard_map/reduce_scatter | solution.py:316
  239.3 1.5 copy-start.4
Sparse Core Ops, SparseCore 0:
  10.3 65.1 all-gather.2
  78.3 125.4 all-gather.4
  239.5 118.3 reduce-scatter.1

commit v7 on v5

--- a/solution.py
+++ b/solution.py
@@ -213,7 +213,6 @@
     send_x = jnp.concatenate(
         [decode_x[picked], jnp.pad(length_code, ((0, 0), (0, 126)))], axis=1
     ).reshape(n_req, CAP, -1)
-    recv_x = lax.all_to_all(send_x, "req", split_axis=0, concat_axis=0, tiled=True)
 
     shift = jnp.mod(send_dest - own_index, n_req)
     source = jnp.mod(own_index - shift, n_req)
@@ -246,7 +245,8 @@
     )
     recv_cache = lax.all_to_all(send_cache, "req", split_axis=0, concat_axis=0, tiled=True)
     prefill_partial = feed_forward_partial(prefill_res, mlp_gain, all_weights)
-    _, recv_cache, recv_x = lax.optimization_barrier((prefill_partial, recv_cache, recv_x))
+    _, recv_cache, send_x = lax.optimization_barrier((prefill_partial, recv_cache, send_x))
+    recv_x = lax.all_to_all(send_x, "req", split_axis=0, concat_axis=0, tiled=True)
     prefill_out = feed_forward_finish(prefill_res, prefill_partial)
     got_row = recv_x.reshape(n_req * CAP, -1)[arrival_order]
     got_x = got_row[:, : decode_x.shape[1]]

time: 377 us -> 380 us (level)
  blocking collectives: 32.6 us -> 38.4 us
    all_to_all x1, waiting for transfers between devices: 57.6 us -> 42.3 us  [shards(): lax.all_to_all(send_cache, 'req', split_axis=0, concat_axis=0, tiled=True)]
    all_gather x1, waiting for transfers between devices: 96.7 us -> 105 us  [feed_forward_partial(): lax.all_gather(mlp_in, 'blk', axis=0, tiled=True)]
    all_to_all x1, waiting for transfers between devices: 0.01 us -> 6.37 us  [shards(): lax.all_to_all(send_x, 'req', split_axis=0, concat_axis=0, tiled=True)]
    all_to_all x1, blocking collectives: 20.6 us -> 26.4 us  [small_feed_forward(): lax.all_to_all(spread, 'blk', split_axis=0, concat_axis=0, tiled=True)]
  transfers between devices with their start and end apart: 5 -> 5, of which waited for: 2 -> 3; matrix products, arithmetic and copies ran while one was open for 38% -> 37% of each run, Pallas kernels for 4% -> 4%
where the time goes in v7:
time: 380 us; the launch traced here: 379 us
  waiting for transfers between devices  153 us (40%)
  local copies, waits for them, and re-layouts  64.8 us (17%)
  matrix products  61 us (16%)
  blocking collectives  38.4 us (10%)
  other arithmetic  22.7 us (6%)
  between operations  14.3 us (4%)
  Pallas kernels  14.1 us (4%)
  starting transfers between devices  10.3 us (3%)
    all_gather x1, waiting for transfers between devices, feed_forward_partial(): lax.all_gather(mlp_in, 'blk', axis=0, tiled=True)  105 us
    all_to_all x1, waiting for transfers between devices, shards(): lax.all_to_all(send_cache, 'req', split_axis=0, concat_axis=0, tiled=True)  42.3 us
    all_to_all x1, blocking collectives, small_feed_forward(): lax.all_to_all(spread, 'blk', split_axis=0, concat_axis=0, tiled=True)  26.4 us
    gather x1, local copies, waits for them, and re-layouts, shards(): pool_rows[send_pages].reshape(n_req, CAP, cache_length, width_per_row)  22.7 us
    dot_general x1, matrix products, feed_forward_partial(): jnp.einsum('nd,dkf->nkf', lax.all_gather(mlp_in, 'blk', axis=0, tiled=Tru...  20.5 us
    dot_general x1, matrix products, feed_forward_partial(): jnp.einsum('nf,df->nd', hidden, all_weights[:, 2, :], preferred_element_t...  15 us
    optimization_barrier x1, local copies, waits for them, and re-layouts, shards(): lax.optimization_barrier((all_weights, prefill_res, send_cache))  14.3 us
    pallas_call x1, Pallas kernels, decode_attend(): pl.pallas_call(decode_kernel, grid_spec=pltpu.PrefetchScalarGridSpec(num_...  14.1 us
  transfers between devices with their start and end apart: 5, of which 3 were waited for; matrix products, arithmetic and copies ran while one was open for 37% of the time, Pallas kernels for 4%

profile of v7, /device:TPU:0, one launch (start us, length us, event | category | flops | bytes accessed | tf_op | source)
XLA Modules:
  0.0 378.8 jit_solution(4463340193237149188)
XLA Ops:
  7.2 1.1 copy.95
  8.3 1.9 pad_maximum_fusion
  10.2 0.7 convert_element_type.125
  10.9 0.7 convert_element_type.127
  11.6 1.4 fusion.20
  13.0 4.9 %convolution_add_fusion.1 = f32[256,2048]{1,0:T(8,128)S(1)} fusion(bf16[1536,2048]{1,0:T(8,128)(2,1)} %param.20, f32[2048]{0:T(1024)S(1)} %convert_element_type.127, bf16[1,1,256,1536]{3,2,1,0:T(8,128)(2,1)} %param.13, f32[1536]{0:T(1024)S(1)} %convert_element_type.125, f32[256]{0:T(256)S(1)} %add_rsqrt_fusion.1), kind=kOutput, calls=%fused_computation.28 | convolution fusion | flops 1612709888 | bytes 9190400 | tf_op jit(solution)/shard_map/dot_general | solution.py:38
  18.0 1.3 slice.139
  19.3 0.6 slice.94
  19.8 0.7 add_convert_fusion.3
  20.5 0.3 multiply_cosine_fusion
  20.8 0.7 copy.97
  21.7 0.8 copy.96
  22.5 3.5 gather_fusion
  26.0 0.3 slice_negate_fusion.1
  26.3 1.3 maximum_multiply_fusion.1
  27.6 1.0 mul.271
  28.7 0.8 fusion.64
  29.5 0.2 copy.99
  29.7 3.1 copy.101
  32.8 1.5 slice_negate_fusion
  34.3 1.3 maximum_multiply_fusion
  35.5 3.1 copy.102
  38.6 1.3 mul.277
  39.9 3.0 copy.100
  42.9 2.2 add_convert_fusion.1
  45.1 0.3 copy.103
  45.4 1.2 copy.98
  46.9 0.6 gather_fusion.1
  47.6 22.7 %gather_fusion.2 = bf16[768,16,512]{2,1,0:T(8,128)(2,1)} fusion(bf16[408,16,512]{2,1,0:T(8,128)(2,1)} %bitcast.181, s32[1024]{0:T(1024)S(1)} %pad_clamp_fusion.2), kind=kCustom, calls=%fused_computation.2 | custom fusion | bytes 25168896 | tf_op jit(solution)/shard_map/gather | solution.py:210
  70.3 0.7 iota_compare_fusion.5
  71.2 1.3 fusion.7
  72.5 1.6 fusion.1
  74.2 2.5 fusion.23
  76.8 1.4 convolution_add_fusion
  78.2 0.2 multiply_reduce_fusion
  78.4 1.1 multiply_convert_fusion
  79.5 14.3 %copy.107 = bf16[1536,3,1120]{0,2,1:T(8,128)(2,1)} copy(bf16[1536,3,1120]{2,0,1:T(8,128)(2,1)} %all-gather.3.cloned.1.call-done) | data formatting | bytes 20643840 | tf_op jit(solution)/shard_map/optimization_barrier | solution.py:243
  93.8 6.5 %all-to-all-start = ((bf16[16,2,384,512]{3,2,1,0:T(8,128)(2,1)}), bf16[16,2,384,512]{3,2,1,0:T(8,128)(2,1)}, u32[]{:S(2)}, u32[]{:S(2)}) async-start(bf16[16,2,384,512]{3,2,1,0:T(8,128)(2,1)} %bitcast.177), calls=%async_computation.1 | async-start | bytes 25165824 | tf_op jit(solution)/shard_map/all_to_all | solution.py:246
  100.4 104.5 %all-gather.5.cloned.1.call-done = bf16[2048,1536]{1,0:T(8,128)(2,1)} async-done(((bf16[256,1536]{1,0:T(8,128)(2,1)}), bf16[2048,1536]{1,0:T(8,128)(2,1)}) %all-gather.5.cloned.1.call-update) | async-done | bytes 6291472 | tf_op jit(solution)/shard_map/all_gather | solution.py:281
  204.9 20.5 %fusion.2 = f32[2048,2,1120]{0,2,1:T(8,128)} fusion(bf16[2048,1536]{1,0:T(8,128)(2,1)} %all-gather.5.cloned.1.call-done, bf16[1536,3,1120]{0,2,1:T(8,128)(2,1)} %copy.107), kind=kOutput, calls=%fused_computation.13 | convolution fusion | flops 14092861440 | bytes 31522816 | tf_op jit(solution)/shard_map/nd,dkf->nkf/dot_general | solution.py:279
  225.4 15.0 %convolution_convert_fusion = bf16[2048,1536]{1,0:T(8,128)(2,1)} fusion(f32[2048,2,1120]{0,2,1:T(8,128)} %fusion.2, bf16[1536,3,1120]{2,0,1:T(8,128)(2,1)} %all-gather.3.cloned.1.call-done), kind=kOutput, calls=%fused_computation.11 | convolution fusion | flops 7063339008 | bytes 28180480 | tf_op jit(solution)/shard_map/nf,df->nd/dot_general | solution.py:286
  240.5 0.6 copy-done.6
  241.1 0.7 gather_fusion.4
  241.9 0.6 gather_fusion.3
  242.6 0.7 reshape.443
  243.6 0.6 broadcast_clamp_fusion.order_ref
  244.2 42.3 %all-to-all-done = bf16[16,2,384,512]{3,2,1,0:T(8,128)(2,1)} async-done(((bf16[16,2,384,512]{3,2,1,0:T(8,128)(2,1)}), bf16[16,2,384,512]{3,2,1,0:T(8,128)(2,1)}, u32[]{:S(2)}, u32[]{:S(2)}) %all-to-all-start) | async-done | bytes 12582944 | tf_op jit(solution)/shard_map/all_to_all | solution.py:246
  286.5 3.7 all-to-all-start.1
  290.2 6.4 %all-to-all-done.1 = bf16[16,2,1664]{2,1,0:T(2,128)(2,1)S(1)} async-done(((bf16[16,2,1664]{2,1,0:T(2,128)(2,1)}), bf16[16,2,1664]{2,1,0:T(2,128)(2,1)S(1)}, u32[]{:S(2)}, u32[]{:S(2)}) %all-to-all-start.1) | async-done | bytes 106528 | tf_op jit(solution)/shard_map/all_to_all | solution.py:249
  296.6 0.6 gather_fusion.5
  297.3 3.8 %convolution_add_fusion.3 = f32[16,2048]{1,0:T(8,128)S(1)} fusion(bf16[1536,2048]{1,0:T(8,128)(2,1)} %param.20, f32[2048]{0:T(1024)S(1)} %convert_element_type.127, f32[1536]{0:T(1024)S(1)} %convert_element_type.125, f32[16]{0:T(128)S(1)} %add_rsqrt_fusion.3, bf16[16,1664]{1,0:T(8,128)(2,1)S(1)} %gather_fusion.5), kind=kOutput, calls=%fused_computation.33 | convolution fusion | flops 100794368 | bytes 6488576 | tf_op jit(solution)/shard_map/dot_general | solution.py:38
  301.2 0.2 convert_reduce_fusion.1
  302.0 0.7 reshape.448.q_ref
  303.0 0.7 fusion.50.length_ref
  303.7 0.7 pad_maximum_fusion.3.kv_ref
  304.3 14.1 %shard_map.148 = (bf16[16,384,512]{2,1,0:T(8,128)(2,1)}, bf16[16,2,6,128]{3,2,1,0:T(8,128)(2,1)}) custom-call(s32[16]{0:T(128)} %broadcast_clamp_fusion.order_ref, s32[16]{0:T(128)} %fusion.50.length_ref, bf16[32,384,512]{2,1,0:T(8,128)(2,1)} %bitcast.40.first_ref.second_ref, bf16[32,384,512]{2,1,0:T(8,128)(2,1)} %bitcast.40.first_ref.second_ref, ...), custom_call_target="tpu_custom_call" | custom-call | tf_op jit(solution)/shard_map/pallas_call | solution.py:125
  318.4 0.9 reshape.449
  319.3 3.2 multiply_reduce_fusion.1
  322.6 26.4 %all_to_all.20 = bf16[8,16,1536]{2,1,0:T(8,128)(2,1)S(1)} all-to-all(bf16[8,16,1536]{2,1,0:T(8,128)(2,1)S(1)} %broadcast_in_dim.60), channel_id=1, replica_groups=mesh['req'=16,'blk'=8] {'blk'}, dimensions={0} | all-to-all | bytes 786432 | tf_op jit(solution)/shard_map/all_to_all | solution.py:296
  349.1 5.0 %fusion.4 = f32[128,2,1120]{0,2,1:T(8,128)S(1)} fusion(bf16[128,1536,1]{1,0,2:T(8,128)(2,1)S(1)} %bitcast.194, bf16[1536,3,1120]{0,2,1:T(8,128)(2,1)} %copy.107), kind=kOutput, calls=%fused_computation.15 | convolution fusion | flops 880803840 | bytes 8421376 | tf_op jit(solution)/shard_map/nd,dkf->nkf/dot_general | solution.py:297
  354.0 3.3 fusion.17
  357.4 12.0 %all_to_all.21 = bf16[8,16,1536]{2,1,0:T(8,128)(2,1)S(1)} all-to-all(bf16[8,16,1536]{2,1,0:T(8,128)(2,1)S(1)} %bitcast.195), channel_id=1, replica_groups=mesh['req'=16,'blk'=8] {'blk'}, dimensions={0} | all-to-all | bytes 786432 | tf_op jit(solution)/shard_map/all_to_all | solution.py:307
  369.4 0.6 fusion.41
  370.1 2.2 fusion.26
  (86 shorter events, 2.8 us)
Async XLA Ops:
  7.2 234.8 %copy-start = (bf16[1,1,16,1536]{3,2,1,0:T(8,128)(2,1)S(1)}, bf16[1,1,16,1536]{3,2,1,0:T(8,128)(2,1)}, u32[]{:S(2)}) copy-start(bf16[1,1,16,1536]{3,2,1,0:T(8,128)(2,1)} %param.14) | copy-start | bytes 147460
  7.2 71.0 %all-gather.3.cloned.1.call-start = ((), (), s32[]{:S(2)}) async-start(), calls=%async_computation.5 | async-start | bytes 11280384 | tf_op jit(solution)/shard_map/all_gather | solution.py:195
  10.2 194.8 %all-gather.5.cloned.1.call-start = ((), (), s32[]{:S(2)}) async-start(), calls=%async_computation.6 | async-start | bytes 7077888 | tf_op jit(solution)/shard_map/all_gather | solution.py:281
  13.0 6.3 %copy-start.5 = (s32[1,1,17]{2,1,0:T(1,128)S(1)}, s32[1,1,17]{2,1,0:T(1,128)}, u32[]{:S(2)}) copy-start(s32[1,1,17]{2,1,0:T(1,128)} %param.17) | copy-start | bytes 208
  13.0 9.5 %copy-start.2 = (s32[1,1,17,24]{3,1,2,0:T(1,128)S(1)}, s32[1,1,17,24]{3,1,2,0:T(1,128)}, u32[]{:S(2)}) copy-start(s32[1,1,17,24]{3,1,2,0:T(1,128)} %param.16) | copy-start | bytes 4900
  38.6 8.0 %copy-start.4 = (s32[1,1,16]{2,1,0:T(1,128)S(1)}, s32[1,1,16]{2,1,0:T(1,128)}, u32[]{:S(2)}) copy-start(s32[1,1,16]{2,1,0:T(1,128)} %param.18) | copy-start | bytes 196
  47.6 22.7 %copy-start.3 = (bf16[1536]{0:T(1024)(128)(2,1)S(1)}, bf16[1536]{0:T(1024)(128)(2,1)}, u32[]{:S(2)}) copy-start(bf16[1536]{0:T(1024)(128)(2,1)} %param.23) | copy-start | bytes 9220
  72.5 4.2 %slice-start = ((s8[4718592]{0:T(1024)(128)(4,1)}), s8[524288]{0:T(1024)(128)(4,1)S(1)}, s32[]{:S(2)}) async-start(s8[4718592]{0:T(1024)(128)(4,1)} %bitcast.178), calls=%async_computation.8 | async-start | bytes 1048576
  74.2 2.6 slice-start.1
  74.2 2.6 copy-start.1
  93.8 192.7 %all-to-all-start = ((bf16[16,2,384,512]{3,2,1,0:T(8,128)(2,1)}), bf16[16,2,384,512]{3,2,1,0:T(8,128)(2,1)}, u32[]{:S(2)}, u32[]{:S(2)}) async-start(bf16[16,2,384,512]{3,2,1,0:T(8,128)(2,1)} %bitcast.177), calls=%async_computation.1 | async-start | bytes 25165824 | tf_op jit(solution)/shard_map/all_to_all | solution.py:246
  100.4 269.7 %reduce-scatter.2.cloned.1.call-start = ((), (), s32[]{:S(2)}) async-start(), calls=%async_computation.7 | async-start | bytes 7077888 | tf_op jit(solution)/shard_map/reduce_scatter | solution.py:315
  240.5 0.7 copy-start.6
  286.5 10.1 %all-to-all-start.1 = ((bf16[16,2,1664]{2,1,0:T(2,128)(2,1)}), bf16[16,2,1664]{2,1,0:T(2,128)(2,1)S(1)}, u32[]{:S(2)}, u32[]{:S(2)}) async-start(bf16[16,2,1664]{2,1,0:T(2,128)(2,1)} %reshape.443), calls=%async_computation.2 | async-start | bytes 212992 | tf_op jit(solution)/shard_map/all_to_all | solution.py:249
Sparse Core Ops, SparseCore 0:
  10.3 65.1 all-gather.2
  79.6 125.2 all-gather.4
  240.6 119.8 reduce-scatter.1

commit v8 on v5

--- a/solution.py
+++ b/solution.py
@@ -11,6 +11,7 @@
 KEY_VALUE_HEADS = 2
 HEAD_SIZE = 128
 CAP = 2
+PER_STEP = 4
 
 
 rms_eps = 1e-06
@@ -86,11 +87,13 @@
     return result.reshape(batch_count, total_rows, QUERY_HEADS * HEAD_SIZE).astype(jnp.bfloat16)
 
 
-def decode_kernel(order_ref, length_ref, first_ref, second_ref, kv_ref, q_ref, new_ref, att_ref):
+def decode_kernel(order_ref, length_ref, *refs):
+    cache_refs = refs[:PER_STEP]
+    kv_ref, q_ref, new_ref, att_ref = refs[PER_STEP:]
     group_width = QUERY_HEADS // KEY_VALUE_HEADS
     key_head_width = KEY_VALUE_HEADS * HEAD_SIZE
-    for half, cache_ref in enumerate((first_ref, second_ref)):
-        limit = length_ref[2 * pl.program_id(0) + half]
+    for half, cache_ref in enumerate(cache_refs):
+        limit = length_ref[PER_STEP * pl.program_id(0) + half]
         rows = cache_ref[...]
         positions = lax.broadcasted_iota(jnp.int32, rows.shape, 0)
         extended = jnp.where(
@@ -121,22 +124,25 @@
     cache_length, width_per_row = recv_cache.shape[1:]
     group_width = QUERY_HEADS // KEY_VALUE_HEADS
     order = jnp.clip(arrival_order, 0, recv_cache.shape[0] - 1)
-    head_block = (2, KEY_VALUE_HEADS, group_width, HEAD_SIZE)
+    head_block = (PER_STEP, KEY_VALUE_HEADS, group_width, HEAD_SIZE)
     new_cache, attended = pl.pallas_call(
         decode_kernel,
         grid_spec=pltpu.PrefetchScalarGridSpec(
             num_scalar_prefetch=2,
-            grid=(count // 2,),
+            grid=(count // PER_STEP,),
             in_specs=[
-                pl.BlockSpec((None, cache_length, width_per_row), lambda p, o, n: (o[2 * p], 0, 0)),
-                pl.BlockSpec(
-                    (None, cache_length, width_per_row), lambda p, o, n: (o[2 * p + 1], 0, 0)
-                ),
-                pl.BlockSpec((2, 1, width_per_row), lambda p, o, n: (p, 0, 0)),
+                *[
+                    pl.BlockSpec(
+                        (None, cache_length, width_per_row),
+                        lambda p, o, n, k=k: (o[PER_STEP * p + k], 0, 0),
+                    )
+                    for k in range(PER_STEP)
+                ],
+                pl.BlockSpec((PER_STEP, 1, width_per_row), lambda p, o, n: (p, 0, 0)),
                 pl.BlockSpec(head_block, lambda p, o, n: (p, 0, 0, 0)),
             ],
             out_specs=[
-                pl.BlockSpec((2, cache_length, width_per_row), lambda p, o, n: (p, 0, 0)),
+                pl.BlockSpec((PER_STEP, cache_length, width_per_row), lambda p, o, n: (p, 0, 0)),
                 pl.BlockSpec(head_block, lambda p, o, n: (p, 0, 0, 0)),
             ],
         ),
@@ -147,8 +153,7 @@
     )(
         order,
         got_length,
-        recv_cache,
-        recv_cache,
+        *([recv_cache] * PER_STEP),
         decode_kv.reshape(count, 1, width_per_row),
         decode_q.reshape(count, KEY_VALUE_HEADS, group_width, HEAD_SIZE),
     )

time: 377 us -> 377 us (level)
  no operation moved by 1% of the time
where the time goes in v8:
time: 377 us; the launch traced here: 375 us
  waiting for transfers between devices  154 us (41%)
  local copies, waits for them, and re-layouts  64.3 us (17%)
  matrix products  61.2 us (16%)
  blocking collectives  32.5 us (9%)
  other arithmetic  22.7 us (6%)
  between operations  14.3 us (4%)
  Pallas kernels  13.7 us (4%)
  starting transfers between devices  12.3 us (3%)
    all_gather x1, waiting for transfers between devices, feed_forward_partial(): lax.all_gather(mlp_in, 'blk', axis=0, tiled=True)  96.6 us
    all_to_all x1, waiting for transfers between devices, shards(): lax.all_to_all(send_cache, 'req', split_axis=0, concat_axis=0, tiled=True)  57.7 us
    gather x1, local copies, waits for them, and re-layouts, shards(): pool_rows[send_pages].reshape(n_req, CAP, cache_length, width_per_row)  22.8 us
    all_to_all x1, blocking collectives, small_feed_forward(): lax.all_to_all(spread, 'blk', split_axis=0, concat_axis=0, tiled=True)  20.5 us
    dot_general x1, matrix products, feed_forward_partial(): jnp.einsum('nd,dkf->nkf', lax.all_gather(mlp_in, 'blk', axis=0, tiled=Tru...  20.5 us
    dot_general x1, matrix products, feed_forward_partial(): jnp.einsum('nf,df->nd', hidden, all_weights[:, 2, :], preferred_element_t...  15 us
    optimization_barrier x1, local copies, waits for them, and re-layouts, shards(): lax.optimization_barrier((all_weights, prefill_res, send_cache))  14.4 us
    pallas_call x1, Pallas kernels, decode_attend(): pl.pallas_call(decode_kernel, grid_spec=pltpu.PrefetchScalarGridSpec(num_...  13.7 us
  transfers between devices with their start and end apart: 5, of which 2 were waited for; matrix products, arithmetic and copies ran while one was open for 38% of the time, Pallas kernels for 4%

profile of v8, /device:TPU:0, one launch (start us, length us, event | category | flops | bytes accessed | tf_op | source)
XLA Modules:
  0.0 375.3 jit_solution(12585700406460115870)
XLA Ops:
  7.2 1.1 copy.95
  8.3 1.9 pad_maximum_fusion
  10.2 0.7 convert_element_type.125
  10.9 0.7 convert_element_type.127
  11.6 1.4 fusion.20
  13.0 4.9 %convolution_add_fusion.1 = f32[256,2048]{1,0:T(8,128)S(1)} fusion(bf16[1536,2048]{1,0:T(8,128)(2,1)} %param.20, f32[2048]{0:T(1024)S(1)} %convert_element_type.127, bf16[1,1,256,1536]{3,2,1,0:T(8,128)(2,1)} %param.13, f32[1536]{0:T(1024)S(1)} %convert_element_type.125, f32[256]{0:T(256)S(1)} %add_rsqrt_fusion.1), kind=kOutput, calls=%fused_computation.28 | convolution fusion | flops 1612709888 | bytes 9190400 | tf_op jit(solution)/shard_map/dot_general | solution.py:39
  18.0 1.3 slice.139
  19.3 0.6 slice.94
  19.9 0.7 add_convert_fusion.3
  20.5 0.3 multiply_cosine_fusion
  20.9 0.7 copy.97
  21.7 0.8 copy.96
  22.5 3.5 gather_fusion
  26.0 0.3 slice_negate_fusion.1
  26.3 1.3 maximum_multiply_fusion.1
  27.6 1.0 mul.271
  28.7 0.8 fusion.64
  29.5 0.2 copy.99
  29.7 3.1 copy.101
  32.8 1.5 slice_negate_fusion
  34.3 1.3 maximum_multiply_fusion
  35.5 3.1 copy.102
  38.6 1.3 mul.277
  39.9 3.0 copy.100
  42.9 2.2 add_convert_fusion.1
  45.1 0.3 copy.103
  45.4 1.2 copy.98
  46.6 0.2 convert_reduce_fusion.3
  46.9 0.6 gather_fusion.1
  47.6 22.8 %gather_fusion.2 = bf16[768,16,512]{2,1,0:T(8,128)(2,1)} fusion(bf16[408,16,512]{2,1,0:T(8,128)(2,1)} %bitcast.181, s32[1024]{0:T(1024)S(1)} %pad_clamp_fusion.2), kind=kCustom, calls=%fused_computation.2 | custom fusion | bytes 25168896 | tf_op jit(solution)/shard_map/gather | solution.py:215
  70.4 0.7 iota_compare_fusion.5
  71.3 1.3 fusion.7
  72.6 1.6 fusion.1
  74.3 2.5 fusion.23
  76.8 1.4 convolution_add_fusion
  78.3 0.2 multiply_reduce_fusion
  78.5 1.1 multiply_convert_fusion
  79.6 0.7 gather_fusion.4
  80.4 0.6 gather_fusion.3
  81.1 0.7 reshape.443
  81.8 6.5 %all-to-all-start.1 = ((bf16[16,2,1664]{2,1,0:T(2,128)(2,1)}), bf16[16,2,1664]{2,1,0:T(2,128)(2,1)S(1)}, u32[]{:S(2)}, u32[]{:S(2)}) async-start(bf16[16,2,1664]{2,1,0:T(2,128)(2,1)} %reshape.443), calls=%async_computation.2 | async-start | bytes 212992 | tf_op jit(solution)/shard_map/all_to_all | solution.py:221
  88.3 14.4 %copy.107 = bf16[1536,3,1120]{0,2,1:T(8,128)(2,1)} copy(bf16[1536,3,1120]{2,0,1:T(8,128)(2,1)} %all-gather.3.cloned.1.call-done) | data formatting | bytes 20643840 | tf_op jit(solution)/shard_map/optimization_barrier | solution.py:249
  102.6 5.7 %all-to-all-start = ((bf16[16,2,384,512]{3,2,1,0:T(8,128)(2,1)}), bf16[16,2,384,512]{3,2,1,0:T(8,128)(2,1)}, u32[]{:S(2)}, u32[]{:S(2)}) async-start(bf16[16,2,384,512]{3,2,1,0:T(8,128)(2,1)} %bitcast.177), calls=%async_computation.1 | async-start | bytes 25165824 | tf_op jit(solution)/shard_map/all_to_all | solution.py:252
  108.4 96.6 %all-gather.5.cloned.1.call-done = bf16[2048,1536]{1,0:T(8,128)(2,1)} async-done(((bf16[256,1536]{1,0:T(8,128)(2,1)}), bf16[2048,1536]{1,0:T(8,128)(2,1)}) %all-gather.5.cloned.1.call-update) | async-done | bytes 6291472 | tf_op jit(solution)/shard_map/all_gather | solution.py:286
  204.9 20.5 %fusion.2 = f32[2048,2,1120]{0,2,1:T(8,128)} fusion(bf16[2048,1536]{1,0:T(8,128)(2,1)} %all-gather.5.cloned.1.call-done, bf16[1536,3,1120]{0,2,1:T(8,128)(2,1)} %copy.107), kind=kOutput, calls=%fused_computation.13 | convolution fusion | flops 14092861440 | bytes 31522816 | tf_op jit(solution)/shard_map/nd,dkf->nkf/dot_general | solution.py:284
  225.4 15.0 %convolution_convert_fusion = bf16[2048,1536]{1,0:T(8,128)(2,1)} fusion(f32[2048,2,1120]{0,2,1:T(8,128)} %fusion.2, bf16[1536,3,1120]{2,0,1:T(8,128)(2,1)} %all-gather.3.cloned.1.call-done), kind=kOutput, calls=%fused_computation.11 | convolution fusion | flops 7063339008 | bytes 28180480 | tf_op jit(solution)/shard_map/nf,df->nd/dot_general | solution.py:291
  240.5 0.2 convert_reduce_fusion.2
  240.8 0.6 broadcast_clamp_fusion.order_ref
  241.4 57.7 %all-to-all-done = bf16[16,2,384,512]{3,2,1,0:T(8,128)(2,1)} async-done(((bf16[16,2,384,512]{3,2,1,0:T(8,128)(2,1)}), bf16[16,2,384,512]{3,2,1,0:T(8,128)(2,1)}, u32[]{:S(2)}, u32[]{:S(2)}) %all-to-all-start) | async-done | bytes 12582944 | tf_op jit(solution)/shard_map/all_to_all | solution.py:252
  299.1 0.6 gather_fusion.5
  299.9 4.0 %convolution_add_fusion.3 = f32[16,2048]{1,0:T(8,128)S(1)} fusion(bf16[1536,2048]{1,0:T(8,128)(2,1)} %param.20, f32[2048]{0:T(1024)S(1)} %convert_element_type.127, f32[1536]{0:T(1024)S(1)} %convert_element_type.125, f32[16]{0:T(128)S(1)} %add_rsqrt_fusion.3, bf16[16,1664]{1,0:T(8,128)(2,1)S(1)} %gather_fusion.5), kind=kOutput, calls=%fused_computation.33 | convolution fusion | flops 100794368 | bytes 6488576 | tf_op jit(solution)/shard_map/dot_general | solution.py:39
  303.9 0.2 convert_reduce_fusion.1
  304.7 0.7 reshape.448.refs_5_
  305.7 0.7 fusion.50.length_ref
  306.4 0.7 pad_maximum_fusion.3.refs_4_
  307.0 13.7 %shard_map.148 = (bf16[16,384,512]{2,1,0:T(8,128)(2,1)}, bf16[16,2,6,128]{3,2,1,0:T(8,128)(2,1)}) custom-call(s32[16]{0:T(128)} %broadcast_clamp_fusion.order_ref, s32[16]{0:T(128)} %fusion.50.length_ref, bf16[32,384,512]{2,1,0:T(8,128)(2,1)} %bitcast.40.refs_0_.refs_1_.refs_2_.refs_3_, bf16[32,384,512]{2,1,0:T(8,128)(2,1)} %bitcast.40.refs_0_.refs_1_.refs_2_.refs_3_, ...), custom_call_target="tpu_custom_call" | custom-call | tf_op jit(solution)/shard_map/pallas_call | solution.py:128
  320.7 0.9 reshape.449
  321.6 3.3 multiply_reduce_fusion.1
  325.0 20.5 %all_to_all.20 = bf16[8,16,1536]{2,1,0:T(8,128)(2,1)S(1)} all-to-all(bf16[8,16,1536]{2,1,0:T(8,128)(2,1)S(1)} %broadcast_in_dim.60), channel_id=1, replica_groups=mesh['req'=16,'blk'=8] {'blk'}, dimensions={0} | all-to-all | bytes 786432 | tf_op jit(solution)/shard_map/all_to_all | solution.py:301
  345.6 5.0 %fusion.4 = f32[128,2,1120]{0,2,1:T(8,128)S(1)} fusion(bf16[128,1536,1]{1,0,2:T(8,128)(2,1)S(1)} %bitcast.194, bf16[1536,3,1120]{0,2,1:T(8,128)(2,1)} %copy.107), kind=kOutput, calls=%fused_computation.15 | convolution fusion | flops 880803840 | bytes 8421376 | tf_op jit(solution)/shard_map/nd,dkf->nkf/dot_general | solution.py:302
  350.5 3.4 fusion.17
  353.9 12.0 %all_to_all.21 = bf16[8,16,1536]{2,1,0:T(8,128)(2,1)S(1)} all-to-all(bf16[8,16,1536]{2,1,0:T(8,128)(2,1)S(1)} %bitcast.195), channel_id=1, replica_groups=mesh['req'=16,'blk'=8] {'blk'}, dimensions={0} | all-to-all | bytes 786432 | tf_op jit(solution)/shard_map/all_to_all | solution.py:312
  365.9 0.6 fusion.41
  366.6 2.2 fusion.26
  (88 shorter events, 2.5 us)
Async XLA Ops:
  7.2 73.3 %copy-start = (bf16[1,1,16,1536]{3,2,1,0:T(8,128)(2,1)S(1)}, bf16[1,1,16,1536]{3,2,1,0:T(8,128)(2,1)}, u32[]{:S(2)}) copy-start(bf16[1,1,16,1536]{3,2,1,0:T(8,128)(2,1)} %param.14) | copy-start | bytes 147460
  7.2 71.1 %all-gather.3.cloned.1.call-start = ((), (), s32[]{:S(2)}) async-start(), calls=%async_computation.5 | async-start | bytes 11280384 | tf_op jit(solution)/shard_map/all_gather | solution.py:200
  10.2 194.8 %all-gather.5.cloned.1.call-start = ((), (), s32[]{:S(2)}) async-start(), calls=%async_computation.6 | async-start | bytes 7077888 | tf_op jit(solution)/shard_map/all_gather | solution.py:286
  13.0 6.3 %copy-start.6 = (s32[1,1,17]{2,1,0:T(1,128)S(1)}, s32[1,1,17]{2,1,0:T(1,128)}, u32[]{:S(2)}) copy-start(s32[1,1,17]{2,1,0:T(1,128)} %param.17) | copy-start | bytes 208
  13.0 9.5 %copy-start.3 = (s32[1,1,17,24]{3,1,2,0:T(1,128)S(1)}, s32[1,1,17,24]{3,1,2,0:T(1,128)}, u32[]{:S(2)}) copy-start(s32[1,1,17,24]{3,1,2,0:T(1,128)} %param.16) | copy-start | bytes 4900
  38.6 8.0 %copy-start.5 = (s32[1,1,16]{2,1,0:T(1,128)S(1)}, s32[1,1,16]{2,1,0:T(1,128)}, u32[]{:S(2)}) copy-start(s32[1,1,16]{2,1,0:T(1,128)} %param.18) | copy-start | bytes 196
  47.6 22.8 %copy-start.4 = (bf16[1536]{0:T(1024)(128)(2,1)S(1)}, bf16[1536]{0:T(1024)(128)(2,1)}, u32[]{:S(2)}) copy-start(bf16[1536]{0:T(1024)(128)(2,1)} %param.23) | copy-start | bytes 9220
  72.6 4.2 %slice-start = ((s8[4718592]{0:T(1024)(128)(4,1)}), s8[524288]{0:T(1024)(128)(4,1)S(1)}, s32[]{:S(2)}) async-start(s8[4718592]{0:T(1024)(128)(4,1)} %bitcast.178), calls=%async_computation.8 | async-start | bytes 1048576
  74.3 2.6 slice-start.1
  74.3 2.6 copy-start.2
  76.8 2.8 copy-start.7
  81.8 20.8 %all-to-all-start.1 = ((bf16[16,2,1664]{2,1,0:T(2,128)(2,1)}), bf16[16,2,1664]{2,1,0:T(2,128)(2,1)S(1)}, u32[]{:S(2)}, u32[]{:S(2)}) async-start(bf16[16,2,1664]{2,1,0:T(2,128)(2,1)} %reshape.443), calls=%async_computation.2 | async-start | bytes 212992 | tf_op jit(solution)/shard_map/all_to_all | solution.py:221
  102.6 196.5 %all-to-all-start = ((bf16[16,2,384,512]{3,2,1,0:T(8,128)(2,1)}), bf16[16,2,384,512]{3,2,1,0:T(8,128)(2,1)}, u32[]{:S(2)}, u32[]{:S(2)}) async-start(bf16[16,2,384,512]{3,2,1,0:T(8,128)(2,1)} %bitcast.177), calls=%async_computation.1 | async-start | bytes 25165824 | tf_op jit(solution)/shard_map/all_to_all | solution.py:252
  108.3 258.3 %reduce-scatter.2.cloned.1.call-start = ((), (), s32[]{:S(2)}) async-start(), calls=%async_computation.7 | async-start | bytes 7077888 | tf_op jit(solution)/shard_map/reduce_scatter | solution.py:320
  345.6 23.2 %copy-start.1 = (bf16[1,1,16,1536]{3,2,1,0:T(8,128)(2,1)S(1)}, bf16[1,1,16,1536]{3,2,1,0:T(8,128)(2,1)}, u32[]{:S(2)}) copy-start(bf16[1,1,16,1536]{3,2,1,0:T(8,128)(2,1)} %param.14) | copy-start | bytes 147460
Sparse Core Ops, SparseCore 0:
  10.3 65.1 all-gather.2
  79.7 125.1 all-gather.4
  240.6 118.2 reduce-scatter.1
